TPU v7x, 32 devices: a whole 2x2x4 slice. The times are simulated.
32 devices in a mesh: grp: 2 (over y), bank: 4 (over z), seg: 4 (over x, core).
Axes of the slice: x: 2, y: 2, z: 4, core: 2. Of those that a mesh axis runs over, the one named last changes fastest.
Arguments:
- strain: bfloat16 [256, 2, 2, 2048], P(('grp', 'bank'), None, None, 'seg'), parts along dimension 0, may hold values from -3 to 3
- region_of: int32 [256], P(('grp', 'bank')), parts along dimension 0, may hold values from 0 to 3, as said below
- templates: bfloat16 [256, 2, 2048], P('bank', None, 'seg'), may hold values from -60 to 60
- reads: int32 [4, 4], replicated, may hold values from 0 to 15, as said below
- edges: int32 [256, 15], replicated, may hold values from 48 to 2000, as said below
Outputs:
- snr_power: float32 [16, 64, 256], P('seg', None, ('grp', 'bank')), parts along dimension 2
- chisq: float32 [16, 64, 256], P('seg', None, ('grp', 'bank')), parts along dimension 2
There are 2 independent parts, one for each index of `grp`. A program takes and returns all parts, laid end to end along the dimension named above; an argument that names none is the same for every part. Nothing has to cross between parts.
Inputs may be any that keep to these rules, and one draw needn't show every extreme that they name: `region_of`: the 32 records of one index of bank name any one region at most 24 times, and in every draw one region is named exactly 24 times by the records of every index of bank. Region r reads only blocks held by indices r - 1, r and r + 1 of bank (block b is held by index b // 4); every region reads at least one block of each neighbouring index that exists. For each template the 15 interior edges rise strictly; the first bin starts at frequency 0 and the last ends at 2048.
All inputs are finite; a program needn't handle non-finite values.
Results may differ from a plain program's by a relative error of at most 0.008.
Values may be sent and summed in bfloat16 or wider, within the bound.
A program may use at most 128 MiB of HBM per device.

v0:
```python
import functools
import math

import jax
import jax.numpy as jnp
import numpy as np
from jax import lax
from jax.experimental import pallas as pl
from jax.experimental.pallas import tpu as pltpu
from jax.sharding import PartitionSpec as P

BLOCK_TPL = 16
BINS = 16
LAGS = 16
TPL = 64
F32 = jnp.float32
BF16 = jnp.bfloat16
NT = (((1,), (1,)), ((), ()))
TN = (((0,), (0,)), ((), ()))
HIGH = lax.Precision.HIGHEST


def round_up(value, step):
    return -(-value // step) * step


def phase_tables(seg_count, nfreq):
    period = 2 * nfreq
    lag = np.arange(LAGS, dtype=np.int64) - LAGS // 2
    turns = np.mod(lag[:, None] * np.arange(nfreq, dtype=np.int64)[None, :], period)
    angle = turns * (2.0 * math.pi / period)
    shape = (seg_count, LAGS // seg_count, nfreq)
    return (
        jnp.asarray(np.cos(angle).reshape(shape), F32),
        jnp.asarray(np.sin(angle).reshape(shape), F32),
    )


def exchange_kernel(
    cap, rec, hot_pad, rest_pad,
    planes_ref, strain_ref, reg_hbm, edges_hbm, cos_ref, sin_ref,
    tpl_all, power_all, bins_ref, hot_lhs, rest_lhs, hot_sel, rest_sel, rest_reg, hot_out,
    strain_all, power_own, bounds_ref, cos_own, sin_own, reg_ref, edges_ref,
    tpl_send, tpl_recv, pow_send, pow_recv, str_send, str_recv, local_sem,
):
    banks, segs = tpl_all.shape[:2]
    grp, bank, seg = lax.axis_index("grp"), lax.axis_index("bank"), lax.axis_index("seg")
    rows, width = planes_ref.shape[1:]
    nfreq = segs * width
    lags = cos_own.shape[0]
    mesh_id = pl.DeviceIdType.MESH
    half = segs // 2
    far = lax.rem(seg + half, segs)
    near = seg + 1 - 2 * lax.rem(seg, 2)
    far_near = lax.rem(near + half, segs)
    mine, other = grp, 1 - grp
    to_far, to_near, to_twin = {"seg": far}, {"seg": near}, {"grp": other}

    small = [
        pltpu.make_async_copy(cos_ref.at[seg], cos_own, local_sem.at[3]),
        pltpu.make_async_copy(sin_ref.at[seg], sin_own, local_sem.at[4]),
        pltpu.make_async_copy(edges_hbm, edges_ref, local_sem.at[5]),
        pltpu.make_async_copy(reg_hbm, reg_ref, local_sem.at[6]),
    ]
    for copy in small:
        copy.start()
    barrier = pltpu.get_barrier_semaphore()
    for off in range(1, banks):
        pl.semaphore_signal(
            barrier, inc=1, device_id={"bank": lax.rem(bank + off, banks)}, device_id_type=mesh_id
        )
    for where in (to_far, to_near, to_twin):
        pl.semaphore_signal(barrier, inc=1, device_id=where, device_id_type=mesh_id)
    pl.semaphore_wait(barrier, banks + 2)

    started = []

    def push(src, dst, send, recv, where):
        copy = pltpu.make_async_remote_copy(
            src_ref=src, dst_ref=dst, send_sem=send, recv_sem=recv,
            device_id=where, device_id_type=mesh_id,
        )
        copy.start()
        started.append(copy)

    def landed(slot, recv):
        pltpu.make_async_remote_copy(
            src_ref=slot, dst_ref=slot, send_sem=recv, recv_sem=recv,
            device_id=to_near, device_id_type=mesh_id,
        ).wait_recv()

    def source(off):
        return lax.rem(bank - off + banks, banks)

    Z, X, Y_OWN, Y_FAR, N_MINE, N_OTHER, N_FAR_MINE, N_FAR_OTHER = range(8)
    holds = {
        Z: (seg, mine), X: (far, mine), Y_OWN: (seg, other), Y_FAR: (far, other),
        N_MINE: (near, mine), N_OTHER: (near, other),
        N_FAR_MINE: (far_near, mine), N_FAR_OTHER: (far_near, other),
    }
    relays = {
        Z: ((X, to_far), (Y_OWN, to_twin), (N_MINE, to_near)),
        X: ((Y_FAR, to_twin), (N_FAR_MINE, to_near)),
        Y_OWN: ((N_OTHER, to_near),),
        Y_FAR: ((N_FAR_OTHER, to_near),),
    }

    def relay(kind, off):
        place, plane = holds[kind]
        slot = tpl_all.at[source(off), place, plane]
        landed(slot, tpl_recv.at[kind, off])
        for way, where in relays.get(kind, ()):
            push(slot, slot, tpl_send.at[way, off], tpl_recv.at[way, off], where)

    P_Z, P_X, P_N, P_FAR_N = range(4)
    pow_holds = {P_Z: seg, P_X: far, P_N: near, P_FAR_N: far_near}
    pow_relays = {P_Z: ((P_X, to_far), (P_N, to_near)), P_X: ((P_FAR_N, to_near),)}

    def pow_relay(kind, off):
        slot = power_all.at[source(off), pow_holds[kind]]
        landed(slot, pow_recv.at[kind, off])
        for way, where in pow_relays.get(kind, ()):
            push(slot, slot, pow_send.at[way, off], pow_recv.at[way, off], where)

    own_plane = planes_ref.at[mine]
    own_slot = tpl_all.at[bank, seg, mine]
    for off in range(1, banks):
        push(
            own_plane, own_slot, tpl_send.at[Z, off], tpl_recv.at[Z, off],
            {"bank": lax.rem(bank + off, banks)},
        )
    push(own_plane, own_slot, tpl_send.at[X, 0], tpl_recv.at[X, 0], to_far)
    own_strain = strain_all.at[0, seg]
    push(strain_ref, own_strain, str_send.at[0], str_recv.at[0], to_far)
    push(strain_ref, own_strain, str_send.at[1], str_recv.at[1], to_near)
    push(own_plane, own_slot, tpl_send.at[N_MINE, 0], tpl_recv.at[N_MINE, 0], to_near)
    push(
        planes_ref.at[other], tpl_all.at[bank, seg, other],
        tpl_send.at[N_OTHER, 0], tpl_recv.at[N_OTHER, 0], to_near,
    )
    own_copies = [
        pltpu.make_async_copy(planes_ref, tpl_all.at[bank, seg], local_sem.at[0]),
        pltpu.make_async_copy(strain_ref, own_strain, local_sem.at[1]),
    ]
    for copy in own_copies:
        copy.start()
    for copy in small:
        copy.wait()

    total_rows = edges_ref.shape[1]
    eye = jnp.where(
        lax.broadcasted_iota(jnp.int32, (128, 128), 0) == lax.broadcasted_iota(jnp.int32, (128, 128), 1),
        1.0, 0.0,
    )
    for first in range(0, total_rows, 128):
        bounds_ref[first : first + 128, :] = lax.dot_general(
            eye, edges_ref[:, first : first + 128].astype(F32), NT,
            precision=HIGH, preferred_element_type=F32,
        )

    def bin_index(bounds, first):
        freq = (
            lax.broadcasted_iota(jnp.int32, (bounds.shape[0], width), 1) + first
        ).astype(F32)
        bin_of = jnp.zeros((bounds.shape[0], width), F32)
        for level in range(BINS - 1):
            bin_of = bin_of + jnp.where(freq >= bounds[:, level : level + 1], 1.0, 0.0)
        return bin_of

    bin_of = bin_index(bounds_ref[pl.ds(pl.multiple_of(bank * rows, 8), rows), :], seg * width)
    real_part = planes_ref[0].astype(F32)
    imag_part = planes_ref[1].astype(F32)
    squares = real_part * real_part + imag_part * imag_part
    ones = jnp.ones((8, width), F32)
    for pair in range(BINS // 2):
        picked = jnp.concatenate(
            [jnp.where(bin_of == float(2 * pair + p), squares, 0.0) for p in range(2)], axis=0
        )
        line = lax.dot_general(ones, picked, NT, precision=HIGH, preferred_element_type=F32)
        power_own[pair : pair + 1, :] = line[0:1, :]
    own_power = pltpu.make_async_copy(power_own, power_all.at[bank, seg], local_sem.at[2])
    own_power.start()
    for off in range(1, banks):
        push(
            power_own, power_all.at[bank, seg], pow_send.at[P_Z, off], pow_recv.at[P_Z, off],
            {"bank": lax.rem(bank + off, banks)},
        )
    push(power_own, power_all.at[bank, seg], pow_send.at[P_X, 0], pow_recv.at[P_X, 0], to_far)
    push(power_own, power_all.at[bank, seg], pow_send.at[P_N, 0], pow_recv.at[P_N, 0], to_near)

    def fill_bins(first, last):
        def one(step, carry):
            at = pl.multiple_of(step * BLOCK_TPL, BLOCK_TPL)
            bounds = bounds_ref[pl.ds(at, BLOCK_TPL), :]
            for s in range(segs):
                bins_ref[pl.ds(at, BLOCK_TPL), s * width : (s + 1) * width] = bin_index(
                    bounds, s * width
                ).astype(BF16)
            return carry

        lax.fori_loop(first, last, one, 0)

    blocks = total_rows // BLOCK_TPL
    for off in range(banks):
        if off:
            relay(Z, off)
            relay(X, off - 1)
        if off == 1:
            landed(strain_all.at[0, far], str_recv.at[0])
            push(
                strain_all.at[0, far], strain_all.at[0, far], str_send.at[2], str_recv.at[2], to_near
            )
        if off > 1:
            relay(Y_OWN, off - 1)
            relay(Y_FAR, off - 2)
        fill_bins(off * blocks // banks, (off + 1) * blocks // banks)
    relay(X, banks - 1)
    relay(Y_OWN, banks - 1)
    relay(Y_FAR, banks - 2)
    for off in range(1, banks):
        pow_relay(P_Z, off)
    landed(strain_all.at[0, near], str_recv.at[1])
    landed(strain_all.at[0, far_near], str_recv.at[2])
    own_copies[1].wait()

    row_idx = lax.broadcasted_iota(jnp.int32, (rec, rec), 0)
    col_idx = lax.broadcasted_iota(jnp.int32, (rec, rec), 1)
    reg_row = reg_ref[0:1, :]
    reg_col = jnp.sum(jnp.where(row_idx == col_idx, reg_row, 0), axis=1, keepdims=True)
    count_row = jnp.sum(jnp.where(reg_col == reg_row, 1, 0), axis=0, keepdims=True)
    hot = jnp.min(jnp.where(count_row >= cap, reg_row, 1 << 20), axis=1, keepdims=True)
    is_hot_col = jnp.where(reg_col == hot, 1, 0)
    is_hot_row = jnp.where(reg_row == hot, 1, 0)
    rank_row = jnp.sum(jnp.where(row_idx < col_idx, is_hot_col, 0), axis=0, keepdims=True)
    rest_row = col_idx[0:1, :] - rank_row
    hot_out[0] = jnp.min(jnp.where(count_row >= cap, reg_row, 1 << 20))
    hot_pick = jnp.where(
        (lax.broadcasted_iota(jnp.int32, (hot_pad, rec), 0) == rank_row) & (is_hot_row == 1), 1, 0
    )
    rest_pick = jnp.where(
        (lax.broadcasted_iota(jnp.int32, (rest_pad, rec), 0) == rest_row) & (is_hot_row == 0), 1, 0
    )
    hot_sel[...] = hot_pick.astype(F32)
    rest_sel[...] = rest_pick.astype(F32)
    rest_reg[...] = jnp.broadcast_to(
        jnp.sum(rest_pick * (reg_row + 1), axis=1, keepdims=True) - 1, rest_reg.shape
    )
    lists = ((hot_pick, hot_lhs, hot_pad), (rest_pick, rest_lhs, rest_pad))
    for s in range(segs):
        if s == segs // 2:
            relay(Y_FAR, banks - 1)
            for off in range(banks):
                pow_relay(P_X, off)
        for pick, lhs_ref, pad in lists:
            sel = pick.astype(F32).astype(BF16)
            at = slice(s * width, (s + 1) * width)
            at_im = slice(nfreq + s * width, nfreq + (s + 1) * width)
            parts = []
            for c in range(2):
                parts.append(
                    jnp.concatenate(
                        [
                            jnp.dot(
                                sel,
                                strain_all[0, s, c, d * rec : (d + 1) * rec, :],
                                preferred_element_type=F32,
                            )
                            for d in range(2)
                        ],
                        axis=0,
                    )
                )
            real_part, imag_part = parts
            for lag in range(lags):
                cosine = cos_own[lag : lag + 1, at]
                sine = sin_own[lag : lag + 1, at]
                rot_re = (real_part * cosine - imag_part * sine).astype(BF16)
                rot_im = (real_part * sine + imag_part * cosine).astype(BF16)
                top = (2 * lag) * 2 * pad
                low = (2 * lag + 1) * 2 * pad
                lhs_ref[top : top + 2 * pad, at] = rot_re
                lhs_ref[top : top + 2 * pad, at_im] = rot_im
                lhs_ref[low : low + 2 * pad, at] = rot_im
                lhs_ref[low : low + 2 * pad, at_im] = -rot_re
    for off in range(banks):
        for kind in (N_MINE, N_OTHER, N_FAR_MINE, N_FAR_OTHER):
            relay(kind, off)
        for kind in (P_N, P_FAR_N):
            pow_relay(kind, off)
    own_copies[0].wait()
    own_power.wait()
    for copy in started:
        copy.wait_send()


def follow_kernel(
    held_blocks,
    reads_ref, hot_ref, hot_lhs, rest_lhs, hot_sel, rest_sel, rest_reg,
    t0_ref, t1_ref, t2_ref, t3_ref, b0_ref, b1_ref, b2_ref, b3_ref, power_ref,
    snr_ref, chi_ref,
    tmat, z_ref, hot_stat, rest_stat,
):
    region = pl.program_id(0)
    segs, _, _, width = t0_ref.shape[1:]
    nfreq = segs * width
    lags = snr_ref.shape[0]
    hot_pad, rest_pad = hot_sel.shape[0], rest_sel.shape[0]
    tpl_refs = (t0_ref, t1_ref, t2_ref, t3_ref)
    bin_refs = (b0_ref, b1_ref, b2_ref, b3_ref)

    @pl.when(region == 0)
    def prepare():
        hot_stat[...] = jnp.zeros_like(hot_stat)
        rest_stat[...] = jnp.zeros_like(rest_stat)

    lane = lax.broadcasted_iota(jnp.int32, (8, 2 * TPL), 1)
    weight = jnp.zeros((8, 2 * TPL), F32)
    for i in range(4):
        block_id = reads_ref[region, i]
        bank, inner = block_id // held_blocks, block_id % held_blocks
        total = power_ref[bank, 0]
        for s in range(1, segs):
            total = total + power_ref[bank, s]
        shift = (i - inner + 2 * held_blocks) * BLOCK_TPL % (2 * TPL)
        moved = pltpu.roll(total, shift, 1)
        weight = jnp.where((lane % TPL) // BLOCK_TPL == i, moved, weight)
    weight = weight + 1e-06
    norm = jnp.sum(weight, axis=0, keepdims=True)
    norm = norm + pltpu.roll(norm, TPL, 1)
    inv_norm = 1.0 / norm
    share = weight * inv_norm
    inv_weight = 1.0 / weight

    def run(lhs_ref, pad, store):
        rows = lhs_ref.shape[0]
        group = 4
        for q in range(BINS // group):
            for g in range(group):
                level = jnp.asarray(q * group + g, BF16)
                for i in range(4):
                    at_row = slice(g * TPL + i * BLOCK_TPL, g * TPL + (i + 1) * BLOCK_TPL)
                    for s in range(segs):
                        inside = (
                            bin_refs[i][:, s * width : (s + 1) * width] == level
                        )
                        for c in range(2):
                            at = slice(c * nfreq + s * width, c * nfreq + (s + 1) * width)
                            tmat[q, at_row, at] = jnp.where(
                                inside, tpl_refs[i][0, s, c], jnp.zeros((), BF16)
                            )
            z_ref[0:rows, q * group * TPL : (q + 1) * group * TPL] = lax.dot_general(
                lhs_ref[...], tmat[q], NT, preferred_element_type=F32
            )
        for lag in range(lags):
            top = (2 * lag) * 2 * pad
            low = (2 * lag + 1) * 2 * pad
            zr = [z_ref[top : top + 2 * pad, j * 128 : (j + 1) * 128] for j in range(BINS // 2)]
            zi = [z_ref[low : low + 2 * pad, j * 128 : (j + 1) * 128] for j in range(BINS // 2)]
            full_re = functools.reduce(jnp.add, zr)
            full_im = functools.reduce(jnp.add, zi)
            full_re = full_re + pltpu.roll(full_re, TPL, 1)
            full_im = full_im + pltpu.roll(full_im, TPL, 1)
            signal = (full_re * full_re + full_im * full_im) * inv_norm
            chi = jnp.zeros_like(signal)
            for j in range(BINS // 2):
                diff_re = zr[j] - share[j : j + 1] * full_re
                diff_im = zi[j] - share[j : j + 1] * full_im
                chi = chi + (diff_re * diff_re + diff_im * diff_im) * inv_weight[j : j + 1]
            chi = (chi + pltpu.roll(chi, TPL, 1)) * (1.0 / (2 * BINS - 2))
            store(lag, signal[:pad] + signal[pad:])
            store(lags + lag, chi[:pad] + chi[pad:])

    def store_hot(at, value):
        hot_stat[at] = value

    def store_rest(at, value):
        rest_stat[at] = jnp.where(rest_reg[...] == region, value, rest_stat[at])

    @pl.when(region == hot_ref[0])
    def on_hot():
        run(hot_lhs, hot_pad, store_hot)

    @pl.when(region != hot_ref[0])
    def on_rest():
        run(rest_lhs, rest_pad, store_rest)

    @pl.when(region == pl.num_programs(0) - 1)
    def finish():
        for which, out_ref in enumerate((snr_ref, chi_ref)):
            for lag in range(lags):
                at = which * lags + lag
                value = lax.dot_general(
                    hot_sel[...], hot_stat[at], TN, precision=HIGH, preferred_element_type=F32
                ) + lax.dot_general(
                    rest_sel[...], rest_stat[at], TN, precision=HIGH, preferred_element_type=F32
                )
                out_ref[lag] = value[:, :TPL]


def per_device(strain, region_of, templates, reads, edges):
    region_count = lax.axis_size("bank")
    seg_count = lax.axis_size("seg")
    rec, _, _, width = strain.shape
    nfreq = width * seg_count
    held_rows = templates.shape[0]
    held_blocks = held_rows // BLOCK_TPL
    cap = 3 * rec // region_count
    hot_pad, rest_pad = round_up(cap, 8), round_up(rec - cap, 8)
    lags = LAGS // seg_count
    planes = jnp.transpose(templates, (1, 0, 2))
    strain_planes = jnp.transpose(strain, (2, 1, 0, 3)).reshape(2, 2 * rec, width)
    cos_tab, sin_tab = phase_tables(seg_count, nfreq)
    reg = region_of.reshape(1, rec)
    rows_hot, rows_rest = lags * 4 * hot_pad, lags * 4 * rest_pad
    vmem = pl.BlockSpec(memory_space=pltpu.VMEM)
    anyw = pl.BlockSpec(memory_space=pl.ANY)
    hbm = pl.BlockSpec(memory_space=pltpu.HBM)
    total_rows = edges.shape[0]

    def struct(shape, dtype):
        return jax.ShapeDtypeStruct(shape, dtype)

    dma = pltpu.SemaphoreType.DMA
    exchanged = pl.pallas_call(
        functools.partial(exchange_kernel, cap, rec, hot_pad, rest_pad),
        out_shape=(
            struct((region_count, seg_count) + planes.shape, BF16),
            struct((region_count, seg_count, BINS // 2, 2 * TPL), F32),
            struct((total_rows, nfreq), BF16),
            struct((rows_hot, 2 * nfreq), BF16),
            struct((rows_rest, 2 * nfreq), BF16),
            struct((hot_pad, rec), F32),
            struct((rest_pad, rec), F32),
            struct((rest_pad, 2 * TPL), jnp.int32),
            struct((1,), jnp.int32),
        ),
        in_specs=[vmem, vmem, hbm, hbm, hbm, hbm],
        out_specs=(anyw, anyw) + (vmem,) * 6 + (pl.BlockSpec(memory_space=pltpu.SMEM),),
        scratch_shapes=[
            pltpu.VMEM((1, seg_count) + strain_planes.shape, BF16),
            pltpu.VMEM((BINS // 2, 2 * TPL), F32),
            pltpu.VMEM((total_rows, BINS - 1), F32),
            pltpu.VMEM((lags, nfreq), F32),
            pltpu.VMEM((lags, nfreq), F32),
            pltpu.VMEM((1, rec), jnp.int32),
            pltpu.VMEM((BINS - 1, total_rows), jnp.int32),
            dma((8, region_count)),
            dma((8, region_count)),
            dma((4, region_count)),
            dma((4, region_count)),
            dma((3,)),
            dma((3,)),
            dma((7,)),
        ],
        compiler_params=pltpu.CompilerParams(
            collective_id=0, has_side_effects=True, vmem_limit_bytes=50 * 1024 * 1024
        ),
        name="exchange",
    )(planes, strain_planes, reg, edges.T, cos_tab, sin_tab)
    tpl_all, power_all, bins_all, hot_lhs, rest_lhs, hot_sel, rest_sel, rest_reg, hot = exchanged

    def tpl_spec(i):
        def index(r, reads_ref, hot_ref):
            block_id = reads_ref[r, i]
            return (block_id // held_blocks, 0, 0, block_id % held_blocks, 0)

        return pl.BlockSpec((1, seg_count, 2, BLOCK_TPL, width), index)

    def bin_spec(i):
        return pl.BlockSpec((BLOCK_TPL, nfreq), lambda r, reads_ref, hot_ref: (reads_ref[r, i], 0))

    def whole(array):
        return pl.BlockSpec(
            array.shape, lambda r, a, b: (0,) * array.ndim, pipeline_mode=pl.Buffered(1)
        )

    out = struct((lags, rec, TPL), F32)
    resident = (hot_lhs, rest_lhs, hot_sel, rest_sel, rest_reg)
    snr, chi = pl.pallas_call(
        functools.partial(follow_kernel, held_blocks),
        out_shape=(out, out),
        grid_spec=pltpu.PrefetchScalarGridSpec(
            num_scalar_prefetch=2,
            grid=(region_count,),
            in_specs=[whole(x) for x in resident]
            + [tpl_spec(i) for i in range(4)]
            + [bin_spec(i) for i in range(4)]
            + [whole(power_all)],
            out_specs=(pl.BlockSpec(out.shape, lambda r, a, b: (0, 0, 0)),) * 2,
            scratch_shapes=[
                pltpu.VMEM((4, 4 * TPL, 2 * nfreq), BF16),
                pltpu.VMEM((max(rows_hot, rows_rest), BINS * TPL), F32),
                pltpu.VMEM((2 * lags, hot_pad, 2 * TPL), F32),
                pltpu.VMEM((2 * lags, rest_pad, 2 * TPL), F32),
            ],
        ),
        compiler_params=pltpu.CompilerParams(
            dimension_semantics=("arbitrary",), vmem_limit_bytes=50 * 1024 * 1024
        ),
        name="follow",
    )(
        reads, hot, *resident, tpl_all, tpl_all, tpl_all, tpl_all,
        bins_all, bins_all, bins_all, bins_all, power_all,
    )
    return jnp.transpose(snr, (0, 2, 1)), jnp.transpose(chi, (0, 2, 1))


def solution(mesh):
    placed = (
        P(("grp", "bank"), None, None, "seg"),
        P(("grp", "bank")),
        P("bank", None, "seg"),
        P(),
        P(),
    )
    return jax.shard_map(
        per_device,
        mesh=mesh,
        in_specs=placed,
        out_specs=(P("seg", None, ("grp", "bank")), P("seg", None, ("grp", "bank"))),
        check_vma=False,
    )
```

profile of v0, /device:TPU:0, one launch (start us, length us, event | category | flops | bytes accessed | tf_op | source)
XLA Modules:
  0.0 53.4 jit_solution(13176167564967162729)
XLA Ops:
  0.6 0.9 %copy.10 = bf16[2,2,32,512]{3,2,1,0:T(8,128)(2,1)S(1)} copy(bf16[2,2,32,512]{3,0,1,2:T(2,128)(2,1)} %bitcast.13) | data formatting | bytes 262144 | tf_op jit(solution)/shard_map/transpose | solution.py:411
  1.6 0.9 %copy.12 = bf16[64,2,512]{2,0,1:T(8,128)(2,1)S(1)} copy(bf16[64,2,512]{2,1,0:T(2,128)(2,1)} %param.9) | data formatting | bytes 262144 | tf_op args[2]
  2.5 0.0 copy-start
  2.5 0.9 %copy-done = f32[4,4,2048]{2,1,0:T(4,128)S(1)} copy-done((f32[4,4,2048]{2,1,0:T(4,128)S(1)}, f32[4,4,2048]{2,1,0:T(4,128)}, u32[]{:S(2)}) %copy-start) | copy-done | bytes 131096
  3.4 0.0 copy-start.1
  3.4 0.9 %copy-done.1 = f32[4,4,2048]{2,1,0:T(4,128)S(1)} copy-done((f32[4,4,2048]{2,1,0:T(4,128)S(1)}, f32[4,4,2048]{2,1,0:T(4,128)}, u32[]{:S(2)}) %copy-start.1) | copy-done | bytes 131096
  4.3 0.0 copy-start.2
  4.3 0.7 %copy-done.2 = s32[256,15]{0,1:T(8,128)S(1)} copy-done((s32[256,15]{0,1:T(8,128)S(1)}, s32[256,15]{0,1:T(8,128)}, u32[]{:S(2)}) %copy-start.2) | copy-done | bytes 15384
  5.0 0.0 copy-start.4
  5.0 0.7 %copy-done.4 = s32[32]{0:T(128)S(1)} copy-done((s32[32]{0:T(128)S(1)}, s32[32]{0:T(128)}, u32[]{:S(2)}) %copy-start.4) | copy-done | bytes 152
  5.7 28.0 %exchange.1 = (bf16[4,4,2,64,512]{4,3,2,1,0:T(8,128)(2,1)}, f32[4,4,8,128]{3,2,1,0:T(8,128)S(1)}, bf16[256,2048]{1,0:T(8,128)(2,1)S(1)}, bf16[384,4096]{1,0:T(8,...) custom-call(bf16[2,64,512]{2,1,0:T(8,128)(2,1)S(1)} %bitcast.10, ...), custom_call_target="tpu_custom_call" | custom-call | tf_op jit(solution)/shard_map/exchange/pallas_call | solution.py:424
  33.7 0.0 copy-start.3
  33.7 0.7 %copy-done.3 = s32[4,4]{1,0:T(4,128)S(1)} copy-done((s32[4,4]{1,0:T(4,128)S(1)}, s32[4,4]{1,0:T(4,128)}, u32[]{:S(2)}) %copy-start.3) | copy-done | bytes 88
  34.4 19.0 %follow.1 = (f32[4,32,64]{2,1,0:T(8,128)}, f32[4,32,64]{2,1,0:T(8,128)}) custom-call(s32[4,4]{1,0:T(4,128)S(1)} %copy-done.3, s32[1]{0:T(128)} %get-tuple-element.13.hot_ref, bf16[384,4096]{1,0:T(8,128)(2,1)} %get-tuple-element.14.hot_lhs, bf16[128,4096]{1,0:T(8,128)(2,1)S(1)} %get-tuple-element.15.rest_lhs, f32[24,32]{1,0:T(8,128)S(1)} %get-tuple-element.16.hot_sel, ...), custom_call_target="tpu_custom_call" | custom-call | tf_op jit(solution)/shard_map/follow/pallas_call | solution.py:479
Async XLA Ops:
  2.5 0.9 %copy-start = (f32[4,4,2048]{2,1,0:T(4,128)S(1)}, f32[4,4,2048]{2,1,0:T(4,128)}, u32[]{:S(2)}) copy-start(f32[4,4,2048]{2,1,0:T(4,128)} %constant.5.clone.sin_ref) | copy-start | bytes 393220
  3.4 0.9 %copy-start.1 = (f32[4,4,2048]{2,1,0:T(4,128)S(1)}, f32[4,4,2048]{2,1,0:T(4,128)}, u32[]{:S(2)}) copy-start(f32[4,4,2048]{2,1,0:T(4,128)} %constant.4.clone.cos_ref) | copy-start | bytes 393220
  4.3 0.7 %copy-start.2 = (s32[256,15]{0,1:T(8,128)S(1)}, s32[256,15]{0,1:T(8,128)}, u32[]{:S(2)}) copy-start(s32[256,15]{0,1:T(8,128)} %param.11) | copy-start | bytes 46084
  5.0 0.7 %copy-start.4 = (s32[32]{0:T(128)S(1)}, s32[32]{0:T(128)}, u32[]{:S(2)}) copy-start(s32[32]{0:T(128)} %param.8) | copy-start | bytes 388
  33.7 0.7 %copy-start.3 = (s32[4,4]{1,0:T(4,128)S(1)}, s32[4,4]{1,0:T(4,128)}, u32[]{:S(2)}) copy-start(s32[4,4]{1,0:T(4,128)} %reads_ref.1) | copy-start | bytes 196
where the time goes:
time: 53.7 us; the launch traced here: 53.4 us
  Pallas kernels  47 us (88%)
  local copies, waits for them, and re-layouts  5.7 us (11%)
  between operations  0.66 us (1%)
    pallas_call x1, Pallas kernels, per_device(): pl.pallas_call(functools.partial(exchange_kernel, cap, rec, hot_pad, rest...  28 us
    pallas_call x1, Pallas kernels, per_device(): pl.pallas_call(functools.partial(follow_kernel, held_blocks), out_shape=(...  19 us
    unnamed x11, local copies, waits for them, and re-layouts  4.77 us

commit v1 on v0

--- a/solution.py
+++ b/solution.py
@@ -13,6 +13,8 @@
 BINS = 16
 LAGS = 16
 TPL = 64
+CHUNK = 128
+SLOTS = 4
 F32 = jnp.float32
 BF16 = jnp.bfloat16
 NT = (((1,), (1,)), ((), ()))
@@ -39,7 +41,7 @@
 def exchange_kernel(
     cap, rec, hot_pad, rest_pad,
     planes_ref, strain_ref, reg_hbm, edges_hbm, cos_ref, sin_ref,
-    tpl_all, power_all, bins_ref, hot_lhs, rest_lhs, hot_sel, rest_sel, rest_reg, hot_out,
+    tpl_all, power_all, code_ref, count_ref, hot_lhs, rest_lhs, hot_sel, rest_sel, rest_reg, scalars,
     strain_all, power_own, bounds_ref, cos_own, sin_own, reg_ref, edges_ref,
     tpl_send, tpl_recv, pow_send, pow_recv, str_send, str_recv, local_sem,
 ):
@@ -164,7 +166,7 @@
         ).astype(F32)
         bin_of = jnp.zeros((bounds.shape[0], width), F32)
         for level in range(BINS - 1):
-            bin_of = bin_of + jnp.where(freq >= bounds[:, level : level + 1], 1.0, 0.0)
+            bin_of = jnp.where(freq >= bounds[:, level : level + 1], level + 1.0, bin_of)
         return bin_of
 
     bin_of = bin_index(bounds_ref[pl.ds(pl.multiple_of(bank * rows, 8), rows), :], seg * width)
@@ -188,17 +190,40 @@
     push(power_own, power_all.at[bank, seg], pow_send.at[P_X, 0], pow_recv.at[P_X, 0], to_far)
     push(power_own, power_all.at[bank, seg], pow_send.at[P_N, 0], pow_recv.at[P_N, 0], to_near)
 
-    def fill_bins(first, last):
+    def fill_codes(first, last):
         def one(step, carry):
             at = pl.multiple_of(step * BLOCK_TPL, BLOCK_TPL)
             bounds = bounds_ref[pl.ds(at, BLOCK_TPL), :]
             for s in range(segs):
-                bins_ref[pl.ds(at, BLOCK_TPL), s * width : (s + 1) * width] = bin_index(
-                    bounds, s * width
-                ).astype(BF16)
+                bin_of = bin_index(bounds, s * width)
+                slot = bin_of - SLOTS * jnp.floor(bin_of * (1.0 / SLOTS))
+                for c in range(width // CHUNK):
+                    here = slice(c * CHUNK, (c + 1) * CHUNK)
+                    past = bin_of[:, here] - bin_of[:, c * CHUNK : c * CHUNK + 1]
+                    code = slot[:, here] + SLOTS * jnp.floor(past * (1.0 / SLOTS))
+                    code_ref[
+                        pl.ds(at, BLOCK_TPL), s * width + c * CHUNK : s * width + (c + 1) * CHUNK
+                    ] = code.astype(BF16)
             return carry
 
         lax.fori_loop(first, last, one, 0)
+
+    chunks = nfreq // CHUNK
+    row = lax.broadcasted_iota(jnp.int32, (2 * chunks, 2 * TPL), 0)
+    mark = jnp.where(row < chunks, row, row - chunks + 1) * CHUNK
+    low_lane = lax.broadcasted_iota(jnp.int32, (2 * chunks, 2 * TPL), 1) < TPL
+    most = jnp.zeros((chunks, 2 * TPL), F32)
+    for pair in range(total_rows // (2 * TPL)):
+        count = jnp.zeros((2 * chunks, 2 * TPL), F32)
+        for level in range(BINS - 1):
+            edge = edges_ref[level : level + 1, pair * 2 * TPL : (pair + 1) * 2 * TPL]
+            count = count + jnp.where(edge <= mark, 1.0, 0.0)
+        most = jnp.maximum(most, count[chunks:] - count[:chunks])
+        count = jnp.where(row == 2 * chunks - 1, float(BINS), count)
+        moved = pltpu.roll(count, TPL, 1)
+        count_ref[2 * pair] = jnp.where(low_lane, count, moved)
+        count_ref[2 * pair + 1] = jnp.where(low_lane, moved, count)
+    scalars[1] = jnp.max(most.astype(jnp.int32)) // SLOTS + 1
 
     blocks = total_rows // BLOCK_TPL
     for off in range(banks):
@@ -213,7 +238,7 @@
         if off > 1:
             relay(Y_OWN, off - 1)
             relay(Y_FAR, off - 2)
-        fill_bins(off * blocks // banks, (off + 1) * blocks // banks)
+        fill_codes(off * blocks // banks, (off + 1) * blocks // banks)
     relay(X, banks - 1)
     relay(Y_OWN, banks - 1)
     relay(Y_FAR, banks - 2)
@@ -233,7 +258,7 @@
     is_hot_row = jnp.where(reg_row == hot, 1, 0)
     rank_row = jnp.sum(jnp.where(row_idx < col_idx, is_hot_col, 0), axis=0, keepdims=True)
     rest_row = col_idx[0:1, :] - rank_row
-    hot_out[0] = jnp.min(jnp.where(count_row >= cap, reg_row, 1 << 20))
+    scalars[0] = jnp.min(jnp.where(count_row >= cap, reg_row, 1 << 20))
     hot_pick = jnp.where(
         (lax.broadcasted_iota(jnp.int32, (hot_pad, rec), 0) == rank_row) & (is_hot_row == 1), 1, 0
     )
@@ -254,7 +279,6 @@
         for pick, lhs_ref, pad in lists:
             sel = pick.astype(F32).astype(BF16)
             at = slice(s * width, (s + 1) * width)
-            at_im = slice(nfreq + s * width, nfreq + (s + 1) * width)
             parts = []
             for c in range(2):
                 parts.append(
@@ -278,10 +302,14 @@
                 rot_im = (real_part * sine + imag_part * cosine).astype(BF16)
                 top = (2 * lag) * 2 * pad
                 low = (2 * lag + 1) * 2 * pad
-                lhs_ref[top : top + 2 * pad, at] = rot_re
-                lhs_ref[top : top + 2 * pad, at_im] = rot_im
-                lhs_ref[low : low + 2 * pad, at] = rot_im
-                lhs_ref[low : low + 2 * pad, at_im] = -rot_re
+                for c in range(width // CHUNK):
+                    here = slice(c * CHUNK, (c + 1) * CHUNK)
+                    base = (s * width // CHUNK + c) * 2 * CHUNK
+                    re_at, im_at = slice(base, base + CHUNK), slice(base + CHUNK, base + 2 * CHUNK)
+                    lhs_ref[top : top + 2 * pad, re_at] = rot_re[:, here]
+                    lhs_ref[top : top + 2 * pad, im_at] = rot_im[:, here]
+                    lhs_ref[low : low + 2 * pad, re_at] = rot_im[:, here]
+                    lhs_ref[low : low + 2 * pad, im_at] = -rot_re[:, here]
     for off in range(banks):
         for kind in (N_MINE, N_OTHER, N_FAR_MINE, N_FAR_OTHER):
             relay(kind, off)
@@ -295,106 +323,170 @@
 
 def follow_kernel(
     held_blocks,
-    reads_ref, hot_ref, hot_lhs, rest_lhs, hot_sel, rest_sel, rest_reg,
-    t0_ref, t1_ref, t2_ref, t3_ref, b0_ref, b1_ref, b2_ref, b3_ref, power_ref,
+    reads_ref, scalars_ref, hot_lhs, rest_lhs, hot_sel, rest_sel, rest_reg,
+    tpl_ref, code_ref, power_ref, count_ref,
     snr_ref, chi_ref,
-    tmat, z_ref, hot_stat, rest_stat,
+    close_ref, acc_ref, sum_ref, total_ref, hot_stat, rest_stat,
 ):
-    region = pl.program_id(0)
-    segs, _, _, width = t0_ref.shape[1:]
-    nfreq = segs * width
+    regions = reads_ref.shape[0]
+    segs, width = tpl_ref.shape[1], tpl_ref.shape[4]
+    chunks = segs * width // CHUNK
     lags = snr_ref.shape[0]
     hot_pad, rest_pad = hot_sel.shape[0], rest_sel.shape[0]
-    tpl_refs = (t0_ref, t1_ref, t2_ref, t3_ref)
-    bin_refs = (b0_ref, b1_ref, b2_ref, b3_ref)
-
-    @pl.when(region == 0)
-    def prepare():
-        hot_stat[...] = jnp.zeros_like(hot_stat)
-        rest_stat[...] = jnp.zeros_like(rest_stat)
-
-    lane = lax.broadcasted_iota(jnp.int32, (8, 2 * TPL), 1)
-    weight = jnp.zeros((8, 2 * TPL), F32)
-    for i in range(4):
-        block_id = reads_ref[region, i]
-        bank, inner = block_id // held_blocks, block_id % held_blocks
-        total = power_ref[bank, 0]
-        for s in range(1, segs):
-            total = total + power_ref[bank, s]
-        shift = (i - inner + 2 * held_blocks) * BLOCK_TPL % (2 * TPL)
-        moved = pltpu.roll(total, shift, 1)
-        weight = jnp.where((lane % TPL) // BLOCK_TPL == i, moved, weight)
-    weight = weight + 1e-06
-    norm = jnp.sum(weight, axis=0, keepdims=True)
-    norm = norm + pltpu.roll(norm, TPL, 1)
-    inv_norm = 1.0 / norm
-    share = weight * inv_norm
-    inv_weight = 1.0 / weight
-
-    def run(lhs_ref, pad, store):
+    lane8 = lax.broadcasted_iota(jnp.int32, (8, 2 * TPL), 1)
+    lane_c = lax.broadcasted_iota(jnp.int32, (2 * chunks, 2 * TPL), 1)
+    upper = jnp.where(lax.broadcasted_iota(jnp.int32, (chunks, 2 * TPL), 1) < TPL, 0.0, 1.0)
+    zero = jnp.zeros((), BF16)
+
+    def blocks_of(region):
+        ids = [reads_ref[region, i] for i in range(4)]
+        return [(b // held_blocks, b % held_blocks, b) for b in ids]
+
+    def region_tables(region, groups):
+        weight = jnp.zeros((8, 2 * TPL), F32)
+        count = jnp.zeros((2 * chunks, 2 * TPL), F32)
+        for i, (bank, inner, _) in enumerate(blocks_of(region)):
+            total = power_ref[bank, 0]
+            for s in range(1, segs):
+                total = total + power_ref[bank, s]
+            shift = (i - inner + 2 * held_blocks) * BLOCK_TPL % (2 * TPL)
+            weight = jnp.where(
+                (lane8 % TPL) // BLOCK_TPL == i, pltpu.roll(total, shift, 1), weight
+            )
+            count = jnp.where(
+                (lane_c % TPL) // BLOCK_TPL == i, pltpu.roll(count_ref[bank], shift, 1), count
+            )
+        weight = weight + 1e-06
+        norm = jnp.sum(weight, axis=0, keepdims=True)
+        inv_norm = 1.0 / (norm + pltpu.roll(norm, TPL, 1))
+        inv_weight = 1.0 / weight
+        for g in range(groups):
+            first = count[:chunks] + float(SLOTS * g)
+            last = jnp.minimum(count[chunks:], first + float(SLOTS))
+            for a in range(2):
+                close = jnp.zeros((chunks, 2 * TPL), F32)
+                for m in range(BINS // SLOTS):
+                    level = upper + float(SLOTS * m + 2 * a)
+                    close = jnp.where(
+                        (level >= first) & (level < last),
+                        inv_weight[2 * m + a : 2 * m + a + 1], close,
+                    )
+                close_ref[2 * g + a] = close
+        return inv_norm
+
+    def matrix(blocks, s, at, code_at, g):
+        code = jnp.concatenate(
+            [code_ref[pl.ds(pl.multiple_of(b * BLOCK_TPL, BLOCK_TPL), BLOCK_TPL), code_at] for _, _, b in blocks], axis=0
+        )
+        planes = [
+            jnp.concatenate(
+                [tpl_ref[bank, s, c, pl.ds(pl.multiple_of(inner * BLOCK_TPL, BLOCK_TPL), BLOCK_TPL), at] for bank, inner, _ in blocks],
+                axis=0,
+            )
+            for c in range(2)
+        ]
+        rows = []
+        for slot in range(SLOTS):
+            inside = code == (g * SLOTS + slot).astype(BF16) if not isinstance(g, int) else code == jnp.asarray(g * SLOTS + slot, BF16)
+            rows.append(jnp.concatenate([jnp.where(inside, plane, zero) for plane in planes], axis=1))
+        return jnp.concatenate(rows, axis=0)
+
+    def step(lhs, close, rows, mat, first):
+        part = lax.dot_general(lhs, mat, NT, preferred_element_type=F32)
+        both = part[:, : 2 * TPL] + part[:, 2 * TPL :]
+        total_ref[:rows] = both if first else total_ref[:rows] + both
+        for a in range(2):
+            here = part[:, a * 2 * TPL : (a + 1) * 2 * TPL]
+            if not first:
+                here = here + acc_ref[a, :rows]
+            term = here * here * close[a]
+            sum_here = term if first else sum_ref[a, :rows] + term
+            sum_ref[a, :rows] = sum_here
+            acc_ref[a, :rows] = jnp.where(close[a] > 0.0, 0.0, here)
+
+    def run_fast(blocks, lhs_ref, rows):
+        for c in range(chunks):
+            s, q = c // (width // CHUNK), c % (width // CHUNK)
+            mat = matrix(
+                blocks, s, slice(q * CHUNK, (q + 1) * CHUNK), slice(c * CHUNK, (c + 1) * CHUNK), 0
+            )
+            close = [close_ref[a, c : c + 1, :] for a in range(2)]
+            step(lhs_ref[:, c * 2 * CHUNK : (c + 1) * 2 * CHUNK], close, rows, mat, c == 0)
+
+    def run_any(blocks, lhs_ref, rows, groups):
+        total_ref[:rows] = jnp.zeros((rows, 2 * TPL), F32)
+        for a in range(2):
+            acc_ref[a, :rows] = jnp.zeros((rows, 2 * TPL), F32)
+            sum_ref[a, :rows] = jnp.zeros((rows, 2 * TPL), F32)
+
+        def one_chunk(c, carry):
+            s, q = c // (width // CHUNK), c % (width // CHUNK)
+            at = pl.ds(pl.multiple_of(q * CHUNK, CHUNK), CHUNK)
+            code_at = pl.ds(pl.multiple_of(c * CHUNK, CHUNK), CHUNK)
+            lhs_at = pl.ds(pl.multiple_of(c * 2 * CHUNK, 2 * CHUNK), 2 * CHUNK)
+
+            def one_group(g, carry):
+                mat = matrix(blocks, s, at, code_at, g)
+                close = [close_ref[2 * g + a, pl.ds(c, 1), :] for a in range(2)]
+                step(lhs_ref[:, lhs_at], close, rows, mat, False)
+                return carry
+
+            return lax.fori_loop(0, groups, one_group, carry)
+
+        lax.fori_loop(0, chunks, one_chunk, 0)
+
+    def run(region, lhs_ref, pad, store):
         rows = lhs_ref.shape[0]
-        group = 4
-        for q in range(BINS // group):
-            for g in range(group):
-                level = jnp.asarray(q * group + g, BF16)
-                for i in range(4):
-                    at_row = slice(g * TPL + i * BLOCK_TPL, g * TPL + (i + 1) * BLOCK_TPL)
-                    for s in range(segs):
-                        inside = (
-                            bin_refs[i][:, s * width : (s + 1) * width] == level
-                        )
-                        for c in range(2):
-                            at = slice(c * nfreq + s * width, c * nfreq + (s + 1) * width)
-                            tmat[q, at_row, at] = jnp.where(
-                                inside, tpl_refs[i][0, s, c], jnp.zeros((), BF16)
-                            )
-            z_ref[0:rows, q * group * TPL : (q + 1) * group * TPL] = lax.dot_general(
-                lhs_ref[...], tmat[q], NT, preferred_element_type=F32
-            )
+        blocks = blocks_of(region)
+        inv_norm = region_tables(region, BINS // SLOTS)
+
+        @pl.when(scalars_ref[1] == 1)
+        def fast():
+            run_fast(blocks, lhs_ref, rows)
+
+        @pl.when(scalars_ref[1] != 1)
+        def general():
+            run_any(blocks, lhs_ref, rows, scalars_ref[1])
+
         for lag in range(lags):
-            top = (2 * lag) * 2 * pad
-            low = (2 * lag + 1) * 2 * pad
-            zr = [z_ref[top : top + 2 * pad, j * 128 : (j + 1) * 128] for j in range(BINS // 2)]
-            zi = [z_ref[low : low + 2 * pad, j * 128 : (j + 1) * 128] for j in range(BINS // 2)]
-            full_re = functools.reduce(jnp.add, zr)
-            full_im = functools.reduce(jnp.add, zi)
-            full_re = full_re + pltpu.roll(full_re, TPL, 1)
-            full_im = full_im + pltpu.roll(full_im, TPL, 1)
-            signal = (full_re * full_re + full_im * full_im) * inv_norm
-            chi = jnp.zeros_like(signal)
-            for j in range(BINS // 2):
-                diff_re = zr[j] - share[j : j + 1] * full_re
-                diff_im = zi[j] - share[j : j + 1] * full_im
-                chi = chi + (diff_re * diff_re + diff_im * diff_im) * inv_weight[j : j + 1]
-            chi = (chi + pltpu.roll(chi, TPL, 1)) * (1.0 / (2 * BINS - 2))
-            store(lag, signal[:pad] + signal[pad:])
-            store(lags + lag, chi[:pad] + chi[pad:])
+            top = lag * 4 * pad
+            full = total_ref[top : top + 4 * pad]
+            full = full + pltpu.roll(full, TPL, 1)
+            energy = sum_ref[0, top : top + 4 * pad] + sum_ref[1, top : top + 4 * pad]
+            signal = full * full * inv_norm
+            signal = (signal[:pad] + signal[pad : 2 * pad]) + (signal[2 * pad : 3 * pad] + signal[3 * pad :])
+            energy = (energy[:pad] + energy[pad : 2 * pad]) + (energy[2 * pad : 3 * pad] + energy[3 * pad :])
+            energy = energy + pltpu.roll(energy, TPL, 1)
+            store(lag, signal)
+            store(lags + lag, (energy - signal) * (1.0 / (2 * BINS - 2)))
 
     def store_hot(at, value):
         hot_stat[at] = value
 
-    def store_rest(at, value):
-        rest_stat[at] = jnp.where(rest_reg[...] == region, value, rest_stat[at])
-
-    @pl.when(region == hot_ref[0])
-    def on_hot():
-        run(hot_lhs, hot_pad, store_hot)
-
-    @pl.when(region != hot_ref[0])
-    def on_rest():
-        run(rest_lhs, rest_pad, store_rest)
-
-    @pl.when(region == pl.num_programs(0) - 1)
-    def finish():
-        for which, out_ref in enumerate((snr_ref, chi_ref)):
-            for lag in range(lags):
-                at = which * lags + lag
-                value = lax.dot_general(
-                    hot_sel[...], hot_stat[at], TN, precision=HIGH, preferred_element_type=F32
-                ) + lax.dot_general(
-                    rest_sel[...], rest_stat[at], TN, precision=HIGH, preferred_element_type=F32
-                )
-                out_ref[lag] = value[:, :TPL]
+    rest_stat[...] = jnp.zeros_like(rest_stat)
+    hot = scalars_ref[0]
+    run(hot, hot_lhs, hot_pad, store_hot)
+
+    def other(i, carry):
+        region = lax.rem(hot + i, regions)
+
+        def store_rest(at, value):
+            rest_stat[at] = jnp.where(rest_reg[...] == region, value, rest_stat[at])
+
+        run(region, rest_lhs, rest_pad, store_rest)
+        return carry
+
+    lax.fori_loop(1, regions, other, 0)
+
+    for which, out_ref in enumerate((snr_ref, chi_ref)):
+        for lag in range(lags):
+            at = which * lags + lag
+            value = lax.dot_general(
+                hot_sel[...], hot_stat[at], TN, precision=HIGH, preferred_element_type=F32
+            ) + lax.dot_general(
+                rest_sel[...], rest_stat[at], TN, precision=HIGH, preferred_element_type=F32
+            )
+            out_ref[lag] = value[:, :TPL]
 
 
 def per_device(strain, region_of, templates, reads, edges):
@@ -415,6 +507,7 @@
     vmem = pl.BlockSpec(memory_space=pltpu.VMEM)
     anyw = pl.BlockSpec(memory_space=pl.ANY)
     hbm = pl.BlockSpec(memory_space=pltpu.HBM)
+    smem = pl.BlockSpec(memory_space=pltpu.SMEM)
     total_rows = edges.shape[0]
 
     def struct(shape, dtype):
@@ -427,15 +520,16 @@
             struct((region_count, seg_count) + planes.shape, BF16),
             struct((region_count, seg_count, BINS // 2, 2 * TPL), F32),
             struct((total_rows, nfreq), BF16),
+            struct((region_count, 2 * nfreq // CHUNK, 2 * TPL), F32),
             struct((rows_hot, 2 * nfreq), BF16),
             struct((rows_rest, 2 * nfreq), BF16),
             struct((hot_pad, rec), F32),
             struct((rest_pad, rec), F32),
             struct((rest_pad, 2 * TPL), jnp.int32),
-            struct((1,), jnp.int32),
+            struct((2,), jnp.int32),
         ),
         in_specs=[vmem, vmem, hbm, hbm, hbm, hbm],
-        out_specs=(anyw, anyw) + (vmem,) * 6 + (pl.BlockSpec(memory_space=pltpu.SMEM),),
+        out_specs=(vmem,) * 9 + (smem,),
         scratch_shapes=[
             pltpu.VMEM((1, seg_count) + strain_planes.shape, BF16),
             pltpu.VMEM((BINS // 2, 2 * TPL), F32),
@@ -453,55 +547,29 @@
             dma((7,)),
         ],
         compiler_params=pltpu.CompilerParams(
-            collective_id=0, has_side_effects=True, vmem_limit_bytes=50 * 1024 * 1024
+            collective_id=0, has_side_effects=True, vmem_limit_bytes=24 * 1024 * 1024
         ),
         name="exchange",
     )(planes, strain_planes, reg, edges.T, cos_tab, sin_tab)
-    tpl_all, power_all, bins_all, hot_lhs, rest_lhs, hot_sel, rest_sel, rest_reg, hot = exchanged
-
-    def tpl_spec(i):
-        def index(r, reads_ref, hot_ref):
-            block_id = reads_ref[r, i]
-            return (block_id // held_blocks, 0, 0, block_id % held_blocks, 0)
-
-        return pl.BlockSpec((1, seg_count, 2, BLOCK_TPL, width), index)
-
-    def bin_spec(i):
-        return pl.BlockSpec((BLOCK_TPL, nfreq), lambda r, reads_ref, hot_ref: (reads_ref[r, i], 0))
-
-    def whole(array):
-        return pl.BlockSpec(
-            array.shape, lambda r, a, b: (0,) * array.ndim, pipeline_mode=pl.Buffered(1)
-        )
-
+    tpl_all, power_all, code_all, count_all, *lists, scalars = exchanged
     out = struct((lags, rec, TPL), F32)
-    resident = (hot_lhs, rest_lhs, hot_sel, rest_sel, rest_reg)
+    rows_max = max(rows_hot, rows_rest)
     snr, chi = pl.pallas_call(
         functools.partial(follow_kernel, held_blocks),
         out_shape=(out, out),
-        grid_spec=pltpu.PrefetchScalarGridSpec(
-            num_scalar_prefetch=2,
-            grid=(region_count,),
-            in_specs=[whole(x) for x in resident]
-            + [tpl_spec(i) for i in range(4)]
-            + [bin_spec(i) for i in range(4)]
-            + [whole(power_all)],
-            out_specs=(pl.BlockSpec(out.shape, lambda r, a, b: (0, 0, 0)),) * 2,
-            scratch_shapes=[
-                pltpu.VMEM((4, 4 * TPL, 2 * nfreq), BF16),
-                pltpu.VMEM((max(rows_hot, rows_rest), BINS * TPL), F32),
-                pltpu.VMEM((2 * lags, hot_pad, 2 * TPL), F32),
-                pltpu.VMEM((2 * lags, rest_pad, 2 * TPL), F32),
-            ],
-        ),
-        compiler_params=pltpu.CompilerParams(
-            dimension_semantics=("arbitrary",), vmem_limit_bytes=50 * 1024 * 1024
-        ),
+        in_specs=[smem, smem] + [vmem] * 9,
+        out_specs=(vmem, vmem),
+        scratch_shapes=[
+            pltpu.VMEM((2 * BINS // SLOTS, nfreq // CHUNK, 2 * TPL), F32),
+            pltpu.VMEM((2, rows_max, 2 * TPL), F32),
+            pltpu.VMEM((2, rows_max, 2 * TPL), F32),
+            pltpu.VMEM((rows_max, 2 * TPL), F32),
+            pltpu.VMEM((2 * lags, hot_pad, 2 * TPL), F32),
+            pltpu.VMEM((2 * lags, rest_pad, 2 * TPL), F32),
+        ],
+        compiler_params=pltpu.CompilerParams(vmem_limit_bytes=24 * 1024 * 1024),
         name="follow",
-    )(
-        reads, hot, *resident, tpl_all, tpl_all, tpl_all, tpl_all,
-        bins_all, bins_all, bins_all, bins_all, power_all,
-    )
+    )(reads, scalars, *lists, tpl_all, code_all, power_all, count_all)
     return jnp.transpose(snr, (0, 2, 1)), jnp.transpose(chi, (0, 2, 1))
 
 

time: 53.7 us -> 40.4 us (0.75)
  Pallas kernels: 47 us -> 33.7 us
    pallas_call x1, Pallas kernels: 19 us -> 7.56 us  [per_device(): pl.pallas_call(functools.partial(follow_kernel, held_blocks), out_shape=(...]
    pallas_call x1, Pallas kernels: 28 us -> 26.2 us  [per_device(): pl.pallas_call(functools.partial(exchange_kernel, cap, rec, hot_pad, rest...]
where the time goes in v1:
time: 40.4 us; the launch traced here: 40.1 us
  Pallas kernels  33.7 us (83%)
  local copies, waits for them, and re-layouts  5.7 us (14%)
  between operations  0.66 us (2%)
    pallas_call x1, Pallas kernels, per_device(): pl.pallas_call(functools.partial(exchange_kernel, cap, rec, hot_pad, rest...  26.2 us
    pallas_call x1, Pallas kernels, per_device(): pl.pallas_call(functools.partial(follow_kernel, held_blocks), out_shape=(...  7.56 us
    unnamed x11, local copies, waits for them, and re-layouts  4.77 us
    transpose x1, local copies, waits for them, and re-layouts, per_device(): jnp.transpose(strain, (2, 1, 0, 3)).reshape(2, 2 * rec, width)  0.93 us

profile of v1, /device:TPU:0, one launch (start us, length us, event | category | flops | bytes accessed | tf_op | source)
XLA Modules:
  0.0 40.1 jit_solution(12014508996468193595)
XLA Ops:
  0.6 0.9 %copy.10 = bf16[2,2,32,512]{3,2,1,0:T(8,128)(2,1)S(1)} copy(bf16[2,2,32,512]{3,0,1,2:T(2,128)(2,1)} %bitcast.13) | data formatting | bytes 262144 | tf_op jit(solution)/shard_map/transpose | solution.py:503
  1.6 0.9 %copy.12 = bf16[64,2,512]{2,0,1:T(8,128)(2,1)S(1)} copy(bf16[64,2,512]{2,1,0:T(2,128)(2,1)} %param.9) | data formatting | bytes 262144 | tf_op args[2]
  2.5 0.0 copy-start
  2.5 0.9 %copy-done = f32[4,4,2048]{2,1,0:T(4,128)S(1)} copy-done((f32[4,4,2048]{2,1,0:T(4,128)S(1)}, f32[4,4,2048]{2,1,0:T(4,128)}, u32[]{:S(2)}) %copy-start) | copy-done | bytes 131096
  3.4 0.0 copy-start.1
  3.4 0.9 %copy-done.1 = f32[4,4,2048]{2,1,0:T(4,128)S(1)} copy-done((f32[4,4,2048]{2,1,0:T(4,128)S(1)}, f32[4,4,2048]{2,1,0:T(4,128)}, u32[]{:S(2)}) %copy-start.1) | copy-done | bytes 131096
  4.3 0.0 copy-start.2
  4.3 0.7 %copy-done.2 = s32[256,15]{0,1:T(8,128)S(1)} copy-done((s32[256,15]{0,1:T(8,128)S(1)}, s32[256,15]{0,1:T(8,128)}, u32[]{:S(2)}) %copy-start.2) | copy-done | bytes 15384
  5.0 0.0 copy-start.4
  5.0 0.7 %copy-done.4 = s32[32]{0:T(128)S(1)} copy-done((s32[32]{0:T(128)S(1)}, s32[32]{0:T(128)}, u32[]{:S(2)}) %copy-start.4) | copy-done | bytes 152
  5.7 26.2 %exchange.1 = (bf16[4,4,2,64,512]{4,3,2,1,0:T(8,128)(2,1)S(1)}, f32[4,4,8,128]{3,2,1,0:T(8,128)S(1)}, bf16[256,2048]{1,0:T(8,128)(2,1)S(1)}, f32[4,32,128]{2,1,0...) custom-call(bf16[2,64,512]{2,1,0:T(8,128)(2,1)S(1)} %bitcast.10, ...), custom_call_target="tpu_custom_call" | custom-call | tf_op jit(solution)/shard_map/exchange/pallas_call | solution.py:517
  31.9 0.0 copy-start.3
  31.9 0.7 %copy-done.3 = s32[4,4]{1,0:T(4,128)S(1)} copy-done((s32[4,4]{1,0:T(4,128)S(1)}, s32[4,4]{1,0:T(4,128)}, u32[]{:S(2)}) %copy-start.3) | copy-done | bytes 88
  32.5 7.6 %follow.1 = (f32[4,32,64]{2,1,0:T(8,128)}, f32[4,32,64]{2,1,0:T(8,128)}) custom-call(s32[4,4]{1,0:T(4,128)S(1)} %copy-done.3, s32[2]{0:T(128)S(1)} %get-tuple-element.14.scalars_ref, bf16[384,4096]{1,0:T(8,128)(2,1)S(1)} %get-tuple-element.15.hot_lhs, bf16[128,4096]{1,0:T(8,128)(2,1)S(1)} %get-tuple-element.16.rest_lhs, ...), custom_call_target="tpu_custom_call" | custom-call | tf_op jit(solution)/shard_map/follow/pallas_call | solution.py:557
Async XLA Ops:
  2.5 0.9 %copy-start = (f32[4,4,2048]{2,1,0:T(4,128)S(1)}, f32[4,4,2048]{2,1,0:T(4,128)}, u32[]{:S(2)}) copy-start(f32[4,4,2048]{2,1,0:T(4,128)} %constant.5.clone.sin_ref) | copy-start | bytes 393220
  3.4 0.9 %copy-start.1 = (f32[4,4,2048]{2,1,0:T(4,128)S(1)}, f32[4,4,2048]{2,1,0:T(4,128)}, u32[]{:S(2)}) copy-start(f32[4,4,2048]{2,1,0:T(4,128)} %constant.4.clone.cos_ref) | copy-start | bytes 393220
  4.3 0.7 %copy-start.2 = (s32[256,15]{0,1:T(8,128)S(1)}, s32[256,15]{0,1:T(8,128)}, u32[]{:S(2)}) copy-start(s32[256,15]{0,1:T(8,128)} %param.11) | copy-start | bytes 46084
  5.0 0.7 %copy-start.4 = (s32[32]{0:T(128)S(1)}, s32[32]{0:T(128)}, u32[]{:S(2)}) copy-start(s32[32]{0:T(128)} %param.8) | copy-start | bytes 388
  31.9 0.7 %copy-start.3 = (s32[4,4]{1,0:T(4,128)S(1)}, s32[4,4]{1,0:T(4,128)}, u32[]{:S(2)}) copy-start(s32[4,4]{1,0:T(4,128)} %reads_ref.1) | copy-start | bytes 196

commit v2 on v0

--- a/solution.py
+++ b/solution.py
@@ -13,6 +13,8 @@
 BINS = 16
 LAGS = 16
 TPL = 64
+CHUNK = 128
+SLOTS = 4
 F32 = jnp.float32
 BF16 = jnp.bfloat16
 NT = (((1,), (1,)), ((), ()))
@@ -24,7 +26,616 @@
     return -(-value // step) * step
 
 
-def phase_tables(seg_count, nfreq):
+def turn(lag, freq, period):
+    quarter = period // 4
+    moved = (freq * lag + quarter // 2) & (period - 1)
+    quadrant = moved // quarter
+    angle = (moved % quarter - quarter // 2).astype(F32) * (2.0 * math.pi / period)
+    sq = angle * angle
+    sine = angle * (1.0 + sq * (-1.0 / 6 + sq * (1.0 / 120 + sq * (-1.0 / 5040 + sq * (1.0 / 362880)))))
+    cosine = 1.0 + sq * (-0.5 + sq * (1.0 / 24 + sq * (-1.0 / 720 + sq * (1.0 / 40320))))
+    odd = quadrant % 2 == 1
+    big, small = jnp.where(odd, sine, cosine), jnp.where(odd, cosine, sine)
+    cos_out = jnp.where((quadrant == 1) | (quadrant == 2), -big, big)
+    sin_out = jnp.where(quadrant >= 2, -small, small)
+    return cos_out, sin_out
+
+
+def follow_up_kernel(
+    cap, rec, hot_pad, rest_pad, held_blocks,
+    planes_ref, strain_ref, reg_hbm, edges_hbm, reads_hbm,
+    snr_ref, chi_ref, most_ref,
+    tpl_own, tpl_far, power_all, code_ref, bounds_ref, count_ref,
+    hot_lhs, rest_lhs, hot_sel, rest_sel, rest_reg, hot_ref,
+    strain_all, power_own, column_ref, cos_own, sin_own, picked_ref, reg_ref, edges_ref, reads_ref,
+    hot_close, rest_close, hot_acc, hot_sum, hot_total, rest_acc, rest_sum, rest_total,
+    hot_stat, rest_stat,
+    tpl_send, tpl_recv, pow_send, pow_recv, str_send, str_recv, local_sem,
+):
+    banks, segs = power_all.shape[:2]
+    grp, bank, seg = lax.axis_index("grp"), lax.axis_index("bank"), lax.axis_index("seg")
+    width = planes_ref.shape[3]
+    rows = held_blocks * BLOCK_TPL
+    nfreq = segs * width
+    lags = LAGS // segs
+    mesh_id = pl.DeviceIdType.MESH
+    half = segs // 2
+    far = lax.rem(seg + half, segs)
+    near = seg + 1 - 2 * lax.rem(seg, 2)
+    far_near = lax.rem(near + half, segs)
+    mine, other = grp, 1 - grp
+    to_far, to_near, to_twin = {"seg": far}, {"seg": near}, {"grp": other}
+
+    up_ok, down_ok = bank < banks - 1, bank > 0
+
+    small = [
+        pltpu.make_async_copy(edges_hbm, edges_ref, local_sem.at[3]),
+        pltpu.make_async_copy(reg_hbm, reg_ref, local_sem.at[4]),
+        pltpu.make_async_copy(reads_hbm, reads_ref, local_sem.at[5]),
+    ]
+    for copy in small:
+        copy.start()
+    barrier = pltpu.get_barrier_semaphore()
+
+    def greet(where):
+        pl.semaphore_signal(barrier, inc=1, device_id=where, device_id_type=mesh_id)
+
+    for where in (to_far, to_near, to_twin):
+        greet(where)
+    pl.when(up_ok)(lambda: greet({"bank": bank + 1}))
+    pl.when(down_ok)(lambda: greet({"bank": bank - 1}))
+    met = 3 + lax.min(bank, 1) + lax.min(banks - 1 - bank, 1)
+    started = []
+
+    def push(describe, condition=None):
+        def start():
+            describe().start()
+
+        def finish():
+            describe().wait_send()
+
+        if condition is None:
+            start()
+            started.append(finish)
+        else:
+            pl.when(condition)(start)
+            started.append(lambda: pl.when(condition)(finish))
+
+    def remote(src, dst, send, recv, where):
+        return pltpu.make_async_remote_copy(
+            src_ref=src, dst_ref=dst, send_sem=send, recv_sem=recv,
+            device_id=where, device_id_type=mesh_id,
+        )
+
+    def landed(slot, recv):
+        remote(slot, slot, recv, recv, to_near).wait_recv()
+
+    def source(side, hops):
+        return bank - hops if side == 0 else bank + hops
+
+    def present(side, hops):
+        return bank >= hops if side == 0 else bank + hops <= banks - 1
+
+    def number(side, hops):
+        return side * banks + hops
+
+    def onward(side):
+        return (up_ok, {"bank": bank + 1}) if side == 0 else (down_ok, {"bank": bank - 1})
+
+    Z, X, X_OTHER, Y_OWN, Y_FAR, N_MINE, N_OTHER, N_FAR_MINE, N_FAR_OTHER = range(9)
+    core, core_near = lax.rem(seg, half), lax.rem(near, half)
+    holds = {
+        Z: (tpl_own, core, mine), X: (tpl_far, core, mine), X_OTHER: (tpl_far, core, other),
+        Y_OWN: (tpl_own, core, other), Y_FAR: (tpl_far, core, other),
+        N_MINE: (tpl_own, core_near, mine), N_OTHER: (tpl_own, core_near, other),
+        N_FAR_MINE: (tpl_far, core_near, mine), N_FAR_OTHER: (tpl_far, core_near, other),
+    }
+    relays = {
+        Z: ((Y_OWN, to_twin), (X, to_far), (N_MINE, to_near)),
+        X: ((Y_FAR, to_twin), (N_FAR_MINE, to_near)),
+        X_OTHER: ((N_FAR_OTHER, to_near),),
+        Y_OWN: ((N_OTHER, to_near),),
+        Y_FAR: ((N_FAR_OTHER, to_near),),
+    }
+    P_Z, P_X, P_N, P_FAR_N = range(4)
+    pow_holds = {P_Z: seg, P_X: far, P_N: near, P_FAR_N: far_near}
+    pow_relays = {P_Z: ((P_X, to_far), (P_N, to_near)), P_X: ((P_FAR_N, to_near),)}
+
+    def landing(way, kind, side, hops):
+        ref, place, plane = holds[kind]
+        if way in (X, X_OTHER):
+            ref = tpl_far
+        return ref.at[source(side, hops), place, plane]
+
+    def tpl_slot(kind, side, hops):
+        ref, place, plane = holds[kind]
+        return ref.at[source(side, hops), place, plane]
+
+    def pow_slot(kind, side, hops):
+        return power_all.at[source(side, hops), pow_holds[kind]]
+
+    def relay(kind, side=0, hops=0, table=(tpl_slot, tpl_send, tpl_recv, relays, Z)):
+        slot, send, recv, ways, first = table
+        at = number(side, hops)
+        here = present(side, hops) if hops else None
+
+        def wait():
+            landed(slot(kind, side, hops), recv.at[kind, at])
+
+        wait() if here is None else pl.when(here)(wait)
+        if kind == first:
+            more, where = onward(side)
+            push(
+                lambda: remote(
+                    slot(kind, side, hops), slot(kind, side, hops),
+                    send.at[kind, at], recv.at[kind, at + 1], where,
+                ),
+                here & more,
+            )
+        for way, where in ways.get(kind, ()):
+            if hops or way != Y_FAR or slot is pow_slot:
+                push(
+                    lambda way=way, where=where: remote(
+                        slot(kind, side, hops),
+                        slot(kind, side, hops) if slot is pow_slot else landing(way, kind, side, hops),
+                        send.at[way, at], recv.at[way, at], where,
+                    ),
+                    here,
+                )
+
+    def pow_relay(kind, side=0, hops=0):
+        relay(kind, side, hops, (pow_slot, pow_send, pow_recv, pow_relays, P_Z))
+
+    own_plane, other_plane = planes_ref.at[mine], planes_ref.at[other]
+    own_slot, other_slot = tpl_own.at[bank, core, mine], tpl_own.at[bank, core, other]
+    there, there_other = tpl_far.at[bank, core, mine], tpl_far.at[bank, core, other]
+    own_strain = strain_all.at[seg]
+
+    def both_ways(src, dst, send, recv, kind):
+        for side in range(2):
+            more, where = onward(side)
+            push(
+                lambda side=side, where=where: remote(
+                    src, dst, send.at[kind, side * banks], recv.at[kind, number(side, 1)], where
+                ),
+                more,
+            )
+
+    own_copy = pltpu.make_async_copy(planes_ref, tpl_own.at[bank, core], local_sem.at[0])
+    own_copy.start()
+
+    def send_own():
+        both_ways(own_plane, own_slot, tpl_send, tpl_recv, Z)
+        send_power()
+        push(lambda: remote(strain_ref, own_strain, str_send.at[0], str_recv.at[0], to_far))
+        push(lambda: remote(strain_ref, own_strain, str_send.at[1], str_recv.at[1], to_near))
+        push(lambda: remote(own_plane, own_slot, tpl_send.at[N_MINE, 0], tpl_recv.at[N_MINE, 0], to_near))
+        push(lambda: remote(other_plane, other_slot, tpl_send.at[N_OTHER, 0], tpl_recv.at[N_OTHER, 0], to_near))
+
+    for copy in small:
+        copy.wait()
+
+    total_rows = edges_ref.shape[1]
+    upper = seg // half
+    chunks = nfreq // CHUNK
+
+    def fill_tables():
+        eye = jnp.where(
+            lax.broadcasted_iota(jnp.int32, (2 * TPL, 2 * TPL), 0)
+            == lax.broadcasted_iota(jnp.int32, (2 * TPL, 2 * TPL), 1),
+            1.0, 0.0,
+        ).astype(BF16)
+        row = lax.broadcasted_iota(jnp.int32, (2 * chunks, 2 * TPL), 0)
+        mark = (jnp.where(row < chunks, row, row - chunks + 1) * CHUNK).astype(F32)
+        low_lane = lax.broadcasted_iota(jnp.int32, (2 * chunks, 2 * TPL), 1) < TPL
+        most = jnp.zeros((chunks, 2 * TPL), F32)
+        down = upper.astype(F32)
+
+        def turned(table):
+            return lax.dot_general(eye, table.astype(BF16), NT, preferred_element_type=F32)
+
+        for pair in range(total_rows // (2 * TPL)):
+            group = slice(pair * 2 * TPL, (pair + 1) * 2 * TPL)
+            edges = edges_ref[:, group].astype(F32)
+            coarse = jnp.floor(edges * (1.0 / 16))
+            bounds_ref[group, : BINS - 1] = turned(coarse) * 16.0 + turned(edges - coarse * 16.0)
+            count = jnp.zeros((2 * chunks, 2 * TPL), F32)
+            for level in range(BINS - 1):
+                count = count + jnp.where(edges[level : level + 1] <= mark, 1.0, 0.0)
+            first = count[:chunks]
+            most = jnp.maximum(most, count[chunks:] - first)
+            places = [first - SLOTS * jnp.floor(first * (1.0 / SLOTS))]
+            for k in range(SLOTS - 1):
+                place = jnp.full((chunks, 2 * TPL), float(CHUNK), F32)
+                for level in range(k, BINS - 1):
+                    place = jnp.where(
+                        first == float(level - k),
+                        jnp.minimum(edges[level : level + 1] - mark[:chunks], float(CHUNK)), place,
+                    )
+                places.append(place)
+            column_ref[group, : SLOTS * chunks] = turned(jnp.concatenate(places, axis=0)).astype(BF16)
+            count = jnp.where(row == 2 * chunks - 1, BINS - down, count)
+            count = jnp.where(row == 0, -down, count)
+            moved = pltpu.roll(count, TPL, 1)
+            count_ref[2 * pair] = jnp.where(low_lane, count, moved)
+            count_ref[2 * pair + 1] = jnp.where(low_lane, moved, count)
+        most_ref[0] = jnp.max(most.astype(jnp.int32))
+
+    def bin_index(bounds, first):
+        freq = (
+            lax.broadcasted_iota(jnp.int32, (bounds.shape[0], width), 1) + first
+        ).astype(F32)
+        bin_of = jnp.zeros((bounds.shape[0], width), F32)
+        for level in range(BINS - 1):
+            bin_of = jnp.where(freq >= bounds[:, level : level + 1], level + 1.0, bin_of)
+        return bin_of
+
+    own_power = pltpu.make_async_copy(power_own, power_all.at[bank, seg], local_sem.at[2])
+
+    def fill_power():
+        bin_of = bin_index(
+            bounds_ref[pl.ds(pl.multiple_of(bank * rows, 8), rows), : BINS - 1], seg * width
+        )
+        real_part = planes_ref[0].reshape(rows, width).astype(F32)
+        imag_part = planes_ref[1].reshape(rows, width).astype(F32)
+        squares = real_part * real_part + imag_part * imag_part
+        ones = jnp.ones((8, 3 * CHUNK), BF16)
+        for pair in range(BINS // 2):
+            sums = []
+            for p in range(2):
+                picked = jnp.where(bin_of == float(2 * pair + p), squares, 0.0)
+                sums.append(
+                    functools.reduce(
+                        jnp.add,
+                        [picked[:, c * CHUNK : (c + 1) * CHUNK] for c in range(width // CHUNK)],
+                    )
+                )
+            value = jnp.concatenate(sums, axis=0)
+            high = value.astype(BF16)
+            left = value - high.astype(F32)
+            middle = left.astype(BF16)
+            low = (left - middle.astype(F32)).astype(BF16)
+            line = lax.dot_general(
+                ones, jnp.concatenate([high, middle, low], axis=1), NT, preferred_element_type=F32
+            )
+            power_own[pair : pair + 1, :] = line[0:1, :]
+
+    def send_power():
+        own_power.start()
+        slot = power_all.at[bank, seg]
+        both_ways(power_own, slot, pow_send, pow_recv, P_Z)
+        push(lambda: remote(power_own, slot, pow_send.at[P_X, 0], pow_recv.at[P_X, 0], to_far))
+        push(lambda: remote(power_own, slot, pow_send.at[P_N, 0], pow_recv.at[P_N, 0], to_near))
+
+    def fill_codes(first, last):
+        freq = lax.broadcasted_iota(jnp.int32, (BLOCK_TPL, CHUNK), 1).astype(F32).astype(BF16)
+        one_b, zero_b, wrap = (jnp.asarray(v, BF16) for v in (1.0, 0.0, float(SLOTS)))
+
+        def one(step, carry):
+            at = pl.multiple_of(step * BLOCK_TPL, BLOCK_TPL)
+            columns = column_ref[pl.ds(at, BLOCK_TPL), : SLOTS * chunks]
+            for c in range(chunks):
+                slot = columns[:, c : c + 1]
+                for k in range(1, SLOTS):
+                    place = columns[:, k * chunks + c : k * chunks + c + 1]
+                    slot = slot + jnp.where(freq >= place, one_b, zero_b)
+                slot = jnp.where(slot >= wrap, slot - wrap, slot)
+                code_ref[step, :, c * CHUNK : (c + 1) * CHUNK] = slot
+            return carry
+
+        lax.fori_loop(first, last, one, 0)
+
+    def fill_turns():
+        shape = (8, nfreq)
+        lag = seg * lags + lax.broadcasted_iota(jnp.int32, shape, 0) - LAGS // 2
+        freq = lax.broadcasted_iota(jnp.int32, shape, 1)
+        cos_own[...], sin_own[...] = turn(lag, freq, 2 * nfreq)
+
+    def pick_lists():
+        row_idx = lax.broadcasted_iota(jnp.int32, (rec, rec), 0)
+        col_idx = lax.broadcasted_iota(jnp.int32, (rec, rec), 1)
+        reg_row = reg_ref[0:1, :]
+        reg_col = jnp.sum(jnp.where(row_idx == col_idx, reg_row, 0), axis=1, keepdims=True)
+        count_row = jnp.sum(jnp.where(reg_col == reg_row, 1, 0), axis=0, keepdims=True)
+        hot = jnp.min(jnp.where(count_row >= cap, reg_row, 1 << 20), axis=1, keepdims=True)
+        is_hot_col = jnp.where(reg_col == hot, 1, 0)
+        is_hot_row = jnp.where(reg_row == hot, 1, 0)
+        rank_row = jnp.sum(jnp.where(row_idx < col_idx, is_hot_col, 0), axis=0, keepdims=True)
+        rest_row = col_idx[0:1, :] - rank_row
+        hot_ref[0] = jnp.min(jnp.where(count_row >= cap, reg_row, 1 << 20))
+        hot_pick = jnp.where(
+            (lax.broadcasted_iota(jnp.int32, (hot_pad, rec), 0) == rank_row) & (is_hot_row == 1), 1, 0
+        )
+        rest_pick = jnp.where(
+            (lax.broadcasted_iota(jnp.int32, (rest_pad, rec), 0) == rest_row) & (is_hot_row == 0), 1, 0
+        )
+        hot_sel[...] = hot_pick.astype(F32)
+        rest_sel[...] = rest_pick.astype(F32)
+        rest_reg[...] = jnp.broadcast_to(
+            jnp.sum(rest_pick * (reg_row + 1), axis=1, keepdims=True) - 1, rest_reg.shape
+        )
+
+    def fill_lhs(s, strain_at):
+        lists = ((hot_sel, hot_lhs, hot_pad, 0), (rest_sel, rest_lhs, rest_pad, 2 * hot_pad))
+        for sel_ref, _, pad, base in lists:
+            sel = sel_ref[...].astype(BF16)
+            for c in range(2):
+                for d in range(2):
+                    picked_ref[c, base + d * pad : base + (d + 1) * pad, :] = jnp.dot(
+                        sel, strain_at(c, d), preferred_element_type=F32
+                    )
+        for q in range(width // CHUNK):
+            here = slice(q * CHUNK, (q + 1) * CHUNK)
+            at = pl.ds(pl.multiple_of(s * width + q * CHUNK, CHUNK), CHUNK)
+            column = (s * (width // CHUNK) + q) * 2 * CHUNK
+            re_at = pl.ds(pl.multiple_of(column, CHUNK), CHUNK)
+            im_at = pl.ds(pl.multiple_of(column + CHUNK, CHUNK), CHUNK)
+            for _, lhs_ref, pad, base in lists:
+                real_part = picked_ref[0, base : base + 2 * pad, here]
+                imag_part = picked_ref[1, base : base + 2 * pad, here]
+                for lag in range(lags):
+                    cosine = cos_own[lag : lag + 1, at]
+                    sine = sin_own[lag : lag + 1, at]
+                    rot_re = (real_part * cosine - imag_part * sine).astype(BF16)
+                    rot_im = (real_part * sine + imag_part * cosine).astype(BF16)
+                    top = (2 * lag) * 2 * pad
+                    low = (2 * lag + 1) * 2 * pad
+                    lhs_ref[top : top + 2 * pad, re_at] = rot_re
+                    lhs_ref[top : top + 2 * pad, im_at] = rot_im
+                    lhs_ref[low : low + 2 * pad, re_at] = rot_im
+                    lhs_ref[low : low + 2 * pad, im_at] = -rot_re
+
+    def landed_strain(s):
+        return lambda c, d: strain_all[s, c, d * rec : (d + 1) * rec, :]
+
+    blocks = total_rows // BLOCK_TPL
+
+    def codes(part):
+        fill_codes(part * blocks // (2 * banks), (part + 1) * blocks // (2 * banks))
+
+    zero = jnp.zeros((), BF16)
+    lane_c = lax.broadcasted_iota(jnp.int32, (2 * chunks, 2 * TPL), 1)
+    second = jnp.where(lax.broadcasted_iota(jnp.int32, (chunks, 2 * TPL), 1) < TPL, 0.0, 1.0)
+
+    def blocks_of(region):
+        ids = [reads_ref[region, i] for i in range(4)]
+        return [(b // held_blocks, b % held_blocks, b) for b in ids]
+
+    def region_weights(region, close_ref):
+        weight = jnp.zeros((8, 2 * TPL), F32)
+        count = jnp.zeros((2 * chunks, 2 * TPL), F32)
+        for i, (home, inner, _) in enumerate(blocks_of(region)):
+            total = power_all[home, 0]
+            for s in range(1, segs):
+                total = total + power_all[home, s]
+            edges_at = count_ref[home]
+            for k in range(held_blocks):
+                shift = (i - k + 2 * held_blocks) * BLOCK_TPL % (2 * TPL)
+                wanted = jnp.where(lane_c % TPL // BLOCK_TPL == i, inner, held_blocks) == k
+                weight = jnp.where(wanted[:8], pltpu.roll(total, shift, 1), weight)
+                count = jnp.where(wanted, pltpu.roll(edges_at, shift, 1), count)
+        weight = weight + 1e-06
+        inv_weight = 1.0 / weight
+        first = count[:chunks] + upper.astype(F32)
+        last = count[chunks:] + upper.astype(F32)
+        for a in range(2):
+            close = jnp.zeros((chunks, 2 * TPL), F32)
+            for m in range(BINS // SLOTS):
+                level = second + float(SLOTS * m + 2 * a)
+                close = jnp.where(
+                    (level >= first) & (level < last), inv_weight[2 * m + a : 2 * m + a + 1], close
+                )
+            close_ref[a] = close
+        norm = jnp.sum(weight, axis=0, keepdims=True)
+        close_ref[2] = jnp.broadcast_to(
+            1.0 / (norm + pltpu.roll(norm, TPL, 1)), (chunks, 2 * TPL)
+        )
+
+    def half_steps(which, region, lhs_ref, close_ref, acc_ref, sum_ref, total_ref):
+        tpl_ref = tpl_own if which == 0 else tpl_far
+        blocks = blocks_of(region)
+        per_half = chunks // 2
+        for step in range(per_half):
+            at_step = which * per_half + step
+            chunk = at_step + upper * (chunks - 1 - 2 * at_step)
+            place = step + upper * (per_half - 1 - 2 * step)
+            s, q = place // (width // CHUNK), lax.rem(place, width // CHUNK)
+            at = pl.ds(pl.multiple_of(q * CHUNK, CHUNK), CHUNK)
+            code_at = pl.ds(pl.multiple_of(chunk * CHUNK, CHUNK), CHUNK)
+            lhs_at = pl.ds(pl.multiple_of(chunk * 2 * CHUNK, 2 * CHUNK), 2 * CHUNK)
+            code = jnp.concatenate(
+                [code_ref[b, :, code_at] for _, _, b in blocks], axis=0
+            )
+            planes = [
+                jnp.concatenate(
+                    [tpl_ref[home, s, c, inner, :, at] for home, inner, _ in blocks], axis=0
+                )
+                for c in range(2)
+            ]
+            matrix = []
+            for slot in range(SLOTS):
+                inside = code == jnp.asarray(slot, BF16)
+                matrix.append(
+                    jnp.concatenate([jnp.where(inside, plane, zero) for plane in planes], axis=1)
+                )
+            part = lax.dot_general(
+                lhs_ref[:, lhs_at], jnp.concatenate(matrix, axis=0), NT, preferred_element_type=F32
+            )
+            fresh = at_step == 0
+            both = part[:, : 2 * TPL] + part[:, 2 * TPL :]
+            total_ref[...] = both if fresh else total_ref[...] + both
+            for a in range(2):
+                close = close_ref[a, pl.ds(chunk, 1), :]
+                here = part[:, a * 2 * TPL : (a + 1) * 2 * TPL]
+                if not fresh:
+                    here = here + acc_ref[a]
+                term = here * here * close
+                sum_ref[a] = term if fresh else sum_ref[a] + term
+                acc_ref[a] = jnp.where(close > 0.0, 0.0, here)
+
+    def finish_list(pad, close_ref, sum_ref, total_ref, store):
+        inv_norm = close_ref[2, 0:1, :]
+        for lag in range(lags):
+            top = lag * 4 * pad
+            full = total_ref[top : top + 4 * pad]
+            full = full + pltpu.roll(full, TPL, 1)
+            energy = sum_ref[0, top : top + 4 * pad] + sum_ref[1, top : top + 4 * pad]
+            signal = full * full * inv_norm
+            signal = (signal[:pad] + signal[pad : 2 * pad]) + (
+                signal[2 * pad : 3 * pad] + signal[3 * pad :]
+            )
+            energy = (energy[:pad] + energy[pad : 2 * pad]) + (
+                energy[2 * pad : 3 * pad] + energy[3 * pad :]
+            )
+            energy = energy + pltpu.roll(energy, TPL, 1)
+            store(lag, signal)
+            store(lags + lag, (energy - signal) * (1.0 / (2 * BINS - 2)))
+
+    kept = rest_acc.shape[0]
+
+    def other_region(i):
+        return lax.rem(hot_ref[0] + i, banks)
+
+    def hot_half(which):
+        if which == 0:
+            region_weights(hot_ref[0], hot_close)
+        half_steps(which, hot_ref[0], hot_lhs, hot_close, hot_acc, hot_sum, hot_total)
+
+    def rest_half(which, i, at):
+        if which == 0:
+            region_weights(other_region(i), rest_close.at[at])
+        half_steps(
+            which, other_region(i), rest_lhs, rest_close.at[at],
+            rest_acc.at[at], rest_sum.at[at], rest_total.at[at],
+        )
+
+    def rest_done(i, at):
+        region = other_region(i)
+
+        def store(where, value):
+            rest_stat[where] = jnp.where(rest_reg[...] == region, value, rest_stat[where])
+
+        finish_list(rest_pad, rest_close.at[at], rest_sum.at[at], rest_total.at[at], store)
+
+    def each_other(body):
+        def one(i, carry):
+            body(i)
+            return carry
+
+        lax.fori_loop(1, banks, one, 0)
+
+    split_rest = kept == banks - 1
+    sides = [(side, hops) for hops in range(1, banks) for side in range(2)]
+    every = [(0, 0)] + sides
+    work = [functools.partial(codes, part) for part in range(2 * banks)]
+
+    def some(count=1):
+        for _ in range(min(count, len(work))):
+            work.pop(0)()
+
+    fill_tables()
+    fill_power()
+    pl.semaphore_wait(barrier, met)
+    send_own()
+    fill_turns()
+    pick_lists()
+    fill_lhs(seg, lambda c, d: strain_ref[c, d * rec : (d + 1) * rec, :])
+    for hops in range(1, banks):
+        for side in range(2):
+            relay(Z, side, hops)
+        for side in range(2):
+            pow_relay(P_Z, side, hops)
+        if hops == 1:
+            push(lambda: remote(own_plane, there, tpl_send.at[X, 0], tpl_recv.at[X, 0], to_far))
+        if hops == 2 or banks == 2:
+            landed(strain_all.at[far], str_recv.at[0])
+            push(
+                lambda: remote(
+                    strain_all.at[far], strain_all.at[far], str_send.at[2], str_recv.at[2], to_near
+                )
+            )
+            landed(strain_all.at[near], str_recv.at[1])
+            fill_lhs(near, landed_strain(near))
+        some()
+    push(
+        lambda: remote(
+            other_plane, there_other, tpl_send.at[X_OTHER, 0], tpl_recv.at[X_OTHER, 0], to_far
+        )
+    )
+    for hops in range(1, banks):
+        for side in range(2):
+            relay(X, side, hops)
+            relay(Y_OWN, side, hops)
+        for side in range(2):
+            pow_relay(P_X, side, hops)
+        some(2 if hops > 1 else 1)
+        if hops == 1:
+            fill_lhs(far, landed_strain(far))
+    some(len(work))
+    landed(strain_all.at[far_near], str_recv.at[2])
+    fill_lhs(far_near, landed_strain(far_near))
+    pow_relay(P_X)
+    for side, hops in every:
+        for kind in (N_MINE, N_OTHER):
+            relay(kind, side, hops)
+        for kind in (P_N, P_FAR_N):
+            pow_relay(kind, side, hops)
+    own_copy.wait()
+    own_power.wait()
+    relay(X)
+    for side in range(2):
+        relay(Y_FAR, side, 1)
+    hot_half(0)
+    for hops in range(2, banks - 1):
+        for side in range(2):
+            relay(Y_FAR, side, hops)
+    if split_rest:
+        for i in range(1, banks - 1):
+            rest_half(0, i, i - 1)
+    relay(X_OTHER)
+    if banks > 2:
+        for side in range(2):
+            relay(Y_FAR, side, banks - 1)
+    if split_rest:
+        rest_half(0, banks - 1, banks - 2)
+    for side, hops in every:
+        for kind in (N_FAR_MINE, N_FAR_OTHER):
+            relay(kind, side, hops)
+    rest_stat[...] = jnp.zeros_like(rest_stat)
+
+    hot_half(1)
+
+    def store_hot(at, value):
+        hot_stat[at] = value
+
+    finish_list(hot_pad, hot_close, hot_sum, hot_total, store_hot)
+    if split_rest:
+        for i in range(1, banks):
+            rest_half(1, i, i - 1)
+            rest_done(i, i - 1)
+    else:
+
+        def whole_region(i):
+            rest_half(0, i, 0)
+            rest_half(1, i, 0)
+            rest_done(i, 0)
+
+        each_other(whole_region)
+
+    for which, out_ref in enumerate((snr_ref, chi_ref)):
+        for lag in range(lags):
+            at = which * lags + lag
+            value = lax.dot_general(
+                hot_sel[...], hot_stat[at], TN, precision=HIGH, preferred_element_type=F32
+            ) + lax.dot_general(
+                rest_sel[...], rest_stat[at], TN, precision=HIGH, preferred_element_type=F32
+            )
+            out_ref[lag] = value[:, :TPL]
+    for finish in started:
+        finish()
+
+
+def any_phase_tables(seg_count, nfreq):
     period = 2 * nfreq
     lag = np.arange(LAGS, dtype=np.int64) - LAGS // 2
     turns = np.mod(lag[:, None] * np.arange(nfreq, dtype=np.int64)[None, :], period)
@@ -36,7 +647,7 @@
     )
 
 
-def exchange_kernel(
+def any_exchange_kernel(
     cap, rec, hot_pad, rest_pad,
     planes_ref, strain_ref, reg_hbm, edges_hbm, cos_ref, sin_ref,
     tpl_all, power_all, bins_ref, hot_lhs, rest_lhs, hot_sel, rest_sel, rest_reg, hot_out,
@@ -293,7 +904,7 @@
         copy.wait_send()
 
 
-def follow_kernel(
+def any_follow_kernel(
     held_blocks,
     reads_ref, hot_ref, hot_lhs, rest_lhs, hot_sel, rest_sel, rest_reg,
     t0_ref, t1_ref, t2_ref, t3_ref, b0_ref, b1_ref, b2_ref, b3_ref, power_ref,
@@ -397,7 +1008,7 @@
                 out_ref[lag] = value[:, :TPL]
 
 
-def per_device(strain, region_of, templates, reads, edges):
+def any_per_device(strain, region_of, templates, reads, edges):
     region_count = lax.axis_size("bank")
     seg_count = lax.axis_size("seg")
     rec, _, _, width = strain.shape
@@ -409,7 +1020,7 @@
     lags = LAGS // seg_count
     planes = jnp.transpose(templates, (1, 0, 2))
     strain_planes = jnp.transpose(strain, (2, 1, 0, 3)).reshape(2, 2 * rec, width)
-    cos_tab, sin_tab = phase_tables(seg_count, nfreq)
+    cos_tab, sin_tab = any_phase_tables(seg_count, nfreq)
     reg = region_of.reshape(1, rec)
     rows_hot, rows_rest = lags * 4 * hot_pad, lags * 4 * rest_pad
     vmem = pl.BlockSpec(memory_space=pltpu.VMEM)
@@ -422,7 +1033,7 @@
 
     dma = pltpu.SemaphoreType.DMA
     exchanged = pl.pallas_call(
-        functools.partial(exchange_kernel, cap, rec, hot_pad, rest_pad),
+        functools.partial(any_exchange_kernel, cap, rec, hot_pad, rest_pad),
         out_shape=(
             struct((region_count, seg_count) + planes.shape, BF16),
             struct((region_count, seg_count, BINS // 2, 2 * TPL), F32),
@@ -453,9 +1064,9 @@
             dma((7,)),
         ],
         compiler_params=pltpu.CompilerParams(
-            collective_id=0, has_side_effects=True, vmem_limit_bytes=50 * 1024 * 1024
+            collective_id=1, has_side_effects=True, vmem_limit_bytes=50 * 1024 * 1024
         ),
-        name="exchange",
+        name="any_exchange",
     )(planes, strain_planes, reg, edges.T, cos_tab, sin_tab)
     tpl_all, power_all, bins_all, hot_lhs, rest_lhs, hot_sel, rest_sel, rest_reg, hot = exchanged
 
@@ -477,7 +1088,7 @@
     out = struct((lags, rec, TPL), F32)
     resident = (hot_lhs, rest_lhs, hot_sel, rest_sel, rest_reg)
     snr, chi = pl.pallas_call(
-        functools.partial(follow_kernel, held_blocks),
+        functools.partial(any_follow_kernel, held_blocks),
         out_shape=(out, out),
         grid_spec=pltpu.PrefetchScalarGridSpec(
             num_scalar_prefetch=2,
@@ -497,12 +1108,96 @@
         compiler_params=pltpu.CompilerParams(
             dimension_semantics=("arbitrary",), vmem_limit_bytes=50 * 1024 * 1024
         ),
-        name="follow",
+        name="any_follow",
     )(
         reads, hot, *resident, tpl_all, tpl_all, tpl_all, tpl_all,
         bins_all, bins_all, bins_all, bins_all, power_all,
     )
     return jnp.transpose(snr, (0, 2, 1)), jnp.transpose(chi, (0, 2, 1))
+
+
+def per_device(strain, region_of, templates, reads, edges):
+    region_count = lax.axis_size("bank")
+    seg_count = lax.axis_size("seg")
+    rec, _, _, width = strain.shape
+    nfreq = width * seg_count
+    held_rows = templates.shape[0]
+    held_blocks = held_rows // BLOCK_TPL
+    cap = 3 * rec // region_count
+    hot_pad, rest_pad = round_up(cap, 8), round_up(rec - cap, 8)
+    lags = LAGS // seg_count
+    planes = jnp.transpose(templates, (1, 0, 2)).reshape(2, held_blocks, BLOCK_TPL, width)
+    strain_planes = jnp.transpose(strain, (2, 1, 0, 3)).reshape(2, 2 * rec, width)
+    reg = region_of.reshape(1, rec)
+    rows_hot, rows_rest = lags * 4 * hot_pad, lags * 4 * rest_pad
+    vmem = pl.BlockSpec(memory_space=pltpu.VMEM)
+    hbm = pl.BlockSpec(memory_space=pltpu.HBM)
+    smem = pl.BlockSpec(memory_space=pltpu.SMEM)
+    total_rows = edges.shape[0]
+    chunks = nfreq // CHUNK
+    kept = region_count - 1 if region_count <= 4 else 1
+
+    def struct(shape, dtype):
+        return jax.ShapeDtypeStruct(shape, dtype)
+
+    dma = pltpu.SemaphoreType.DMA
+    half_shape = (region_count, seg_count // 2) + planes.shape
+    out = struct((lags, rec, TPL), F32)
+    snr, chi, most = pl.pallas_call(
+        functools.partial(follow_up_kernel, cap, rec, hot_pad, rest_pad, held_blocks),
+        out_shape=(out, out, struct((1,), jnp.int32)),
+        in_specs=[vmem, vmem, hbm, hbm, hbm],
+        out_specs=(vmem, vmem, smem),
+        scratch_shapes=[
+            pltpu.VMEM(half_shape, BF16),
+            pltpu.VMEM(half_shape, BF16),
+            pltpu.VMEM((region_count, seg_count, BINS // 2, 2 * TPL), F32),
+            pltpu.VMEM((total_rows // BLOCK_TPL, BLOCK_TPL, nfreq), BF16),
+            pltpu.VMEM((total_rows, 2 * TPL), F32),
+            pltpu.VMEM((region_count, 2 * chunks, 2 * TPL), F32),
+            pltpu.VMEM((rows_hot, 2 * nfreq), BF16),
+            pltpu.VMEM((rows_rest, 2 * nfreq), BF16),
+            pltpu.VMEM((hot_pad, rec), F32),
+            pltpu.VMEM((rest_pad, rec), F32),
+            pltpu.VMEM((rest_pad, 2 * TPL), jnp.int32),
+            pltpu.SMEM((1,), jnp.int32),
+            pltpu.VMEM((seg_count,) + strain_planes.shape, BF16),
+            pltpu.VMEM((BINS // 2, 2 * TPL), F32),
+            pltpu.VMEM((total_rows, 2 * TPL), BF16),
+            pltpu.VMEM((8, nfreq), F32),
+            pltpu.VMEM((8, nfreq), F32),
+            pltpu.VMEM((2, 2 * (hot_pad + rest_pad), width), F32),
+            pltpu.VMEM((1, rec), jnp.int32),
+            pltpu.VMEM((BINS - 1, total_rows), jnp.int32),
+            pltpu.SMEM(reads.shape, jnp.int32),
+            pltpu.VMEM((3, chunks, 2 * TPL), F32),
+            pltpu.VMEM((kept, 3, chunks, 2 * TPL), F32),
+            pltpu.VMEM((2, rows_hot, 2 * TPL), F32),
+            pltpu.VMEM((2, rows_hot, 2 * TPL), F32),
+            pltpu.VMEM((rows_hot, 2 * TPL), F32),
+            pltpu.VMEM((kept, 2, rows_rest, 2 * TPL), F32),
+            pltpu.VMEM((kept, 2, rows_rest, 2 * TPL), F32),
+            pltpu.VMEM((kept, rows_rest, 2 * TPL), F32),
+            pltpu.VMEM((2 * lags, hot_pad, 2 * TPL), F32),
+            pltpu.VMEM((2 * lags, rest_pad, 2 * TPL), F32),
+            dma((9, 2 * region_count)),
+            dma((9, 2 * region_count)),
+            dma((4, 2 * region_count)),
+            dma((4, 2 * region_count)),
+            dma((3,)),
+            dma((3,)),
+            dma((6,)),
+        ],
+        compiler_params=pltpu.CompilerParams(
+            collective_id=0, has_side_effects=True, vmem_limit_bytes=48 * 1024 * 1024
+        ),
+        name="follow_up",
+    )(planes, strain_planes, reg, edges.T, reads)
+    done = jnp.transpose(snr, (0, 2, 1)), jnp.transpose(chi, (0, 2, 1))
+    return lax.cond(
+        most[0] < SLOTS, lambda: done,
+        lambda: any_per_device(strain, region_of, templates, reads, edges),
+    )
 
 
 def solution(mesh):

time: 53.7 us -> 35.1 us (0.65)
  Pallas kernels: 47 us -> 30.3 us
  local copies, waits for them, and re-layouts: 5.7 us -> 3.11 us
  between operations: 0.66 us -> 1.21 us
    pallas_call x2 -> x1, Pallas kernels: 47 us -> 30.3 us  [per_device(): pl.pallas_call(functools.partial(follow_up_kernel, cap, rec, hot_pad, res...]
    unnamed x11 -> x2, local copies, waits for them, and re-layouts: 4.77 us -> 1.26 us
    transpose x0 -> x1, local copies, waits for them, and re-layouts: none -> 0.92 us  [per_device(): jnp.transpose(templates, (1, 0, 2))]
where the time goes in v2:
time: 35.1 us; the launch traced here: 34.8 us
  Pallas kernels  30.3 us (86%)
  local copies, waits for them, and re-layouts  3.11 us (9%)
  between operations  1.21 us (3%)
    pallas_call x1, Pallas kernels, per_device(): pl.pallas_call(functools.partial(follow_up_kernel, cap, rec, hot_pad, res...  30.3 us
    unnamed x2, local copies, waits for them, and re-layouts  1.26 us
    transpose x1, local copies, waits for them, and re-layouts, per_device(): jnp.transpose(strain, (2, 1, 0, 3)).reshape(2, 2 * rec, width)  0.93 us
    transpose x1, local copies, waits for them, and re-layouts, per_device(): jnp.transpose(templates, (1, 0, 2))  0.92 us

profile of v2, /device:TPU:0, one launch (start us, length us, event | category | flops | bytes accessed | tf_op | source)
XLA Modules:
  0.0 34.8 jit_solution(12936360624814045560)
XLA Ops:
  0.6 0.9 %copy.19 = bf16[2,64,512]{2,1,0:T(8,128)(2,1)S(1)} copy(bf16[2,64,512]{2,0,1:T(2,128)(2,1)} %bitcast.23) | data formatting | bytes 262144 | tf_op jit(solution)/shard_map/transpose | solution.py:1129
  1.6 0.9 %copy.20 = bf16[2,2,32,512]{3,2,1,0:T(8,128)(2,1)S(1)} copy(bf16[2,2,32,512]{3,0,1,2:T(2,128)(2,1)} %bitcast.24) | data formatting | bytes 262144 | tf_op jit(solution)/shard_map/transpose | solution.py:1130
  2.5 30.3 %follow_up.1 = (f32[4,32,64]{2,1,0:T(8,128)S(1)}, f32[4,32,64]{2,1,0:T(8,128)S(1)}, s32[1]{0:T(128)}) custom-call(bf16[2,4,16,512]{3,2,1,0:T(8,128)(2,1)S(1)} %bitcast.21, bf16[2,64,512]{2,1,0:T(8,128)(2,1)S(1)} %bitcast.22, s32[1,32]{1,0:T(1,128)} %bitcast.31, s32[15,256]{1,0:T(8,128)} %bitcast.25, s32[4,4]{1,0:T(4,128)} %reads_hbm.1), custom_call_target="tpu_custom_call" | custom-call | tf_op jit(solution)/shard_map/follow_up/pallas_call | solution.py:1146
  33.4 0.2 conditional.1
  33.6 0.6 %copy.31 = f32[4,64,32]{1,2,0:T(8,128)} copy(f32[4,64,32]{1,2,0:T(8,128)S(1)} %get-tuple-element.84) | data formatting | bytes 65536
  34.2 0.6 %copy.32 = f32[4,64,32]{1,2,0:T(8,128)} copy(f32[4,64,32]{1,2,0:T(8,128)S(1)} %get-tuple-element.85) | data formatting | bytes 65536

commit v3 on v2

--- a/solution.py
+++ b/solution.py
@@ -49,8 +49,8 @@
     hot_lhs, rest_lhs, hot_sel, rest_sel, rest_reg, hot_ref,
     strain_all, power_own, column_ref, cos_own, sin_own, picked_ref, reg_ref, edges_ref, reads_ref,
     hot_close, rest_close, hot_acc, hot_sum, hot_total, rest_acc, rest_sum, rest_total,
-    hot_stat, rest_stat,
-    tpl_send, tpl_recv, pow_send, pow_recv, str_send, str_recv, local_sem,
+    stat_ref,
+    tpl_send, tpl_recv, pow_send, pow_recv, str_send, str_recv, code_send, code_recv, local_sem,
 ):
     banks, segs = power_all.shape[:2]
     grp, bank, seg = lax.axis_index("grp"), lax.axis_index("bank"), lax.axis_index("seg")
@@ -206,14 +206,11 @@
 
     def send_own():
         both_ways(own_plane, own_slot, tpl_send, tpl_recv, Z)
-        send_power()
         push(lambda: remote(strain_ref, own_strain, str_send.at[0], str_recv.at[0], to_far))
         push(lambda: remote(strain_ref, own_strain, str_send.at[1], str_recv.at[1], to_near))
         push(lambda: remote(own_plane, own_slot, tpl_send.at[N_MINE, 0], tpl_recv.at[N_MINE, 0], to_near))
         push(lambda: remote(other_plane, other_slot, tpl_send.at[N_OTHER, 0], tpl_recv.at[N_OTHER, 0], to_near))
 
-    for copy in small:
-        copy.wait()
 
     total_rows = edges_ref.shape[1]
     upper = seg // half
@@ -307,11 +304,12 @@
         push(lambda: remote(power_own, slot, pow_send.at[P_X, 0], pow_recv.at[P_X, 0], to_far))
         push(lambda: remote(power_own, slot, pow_send.at[P_N, 0], pow_recv.at[P_N, 0], to_near))
 
-    def fill_codes(first, last):
+    def fill_codes(first, count):
         freq = lax.broadcasted_iota(jnp.int32, (BLOCK_TPL, CHUNK), 1).astype(F32).astype(BF16)
         one_b, zero_b, wrap = (jnp.asarray(v, BF16) for v in (1.0, 0.0, float(SLOTS)))
 
         def one(step, carry):
+            step = first + step
             at = pl.multiple_of(step * BLOCK_TPL, BLOCK_TPL)
             columns = column_ref[pl.ds(at, BLOCK_TPL), : SLOTS * chunks]
             for c in range(chunks):
@@ -323,7 +321,7 @@
                 code_ref[step, :, c * CHUNK : (c + 1) * CHUNK] = slot
             return carry
 
-        lax.fori_loop(first, last, one, 0)
+        lax.fori_loop(0, count, one, 0)
 
     def fill_turns():
         shape = (8, nfreq)
@@ -390,8 +388,23 @@
 
     blocks = total_rows // BLOCK_TPL
 
+    per_part = blocks // (2 * banks)
+
+    def codes_at(of, part):
+        return code_ref.at[pl.ds((of * banks + part) * per_part, per_part)]
+
     def codes(part):
-        fill_codes(part * blocks // (2 * banks), (part + 1) * blocks // (2 * banks))
+        fill_codes((core * banks + part) * per_part, per_part)
+        if part:
+            send_codes(part - 1)
+
+    def send_codes(part):
+        push(
+            lambda: remote(
+                codes_at(core, part), codes_at(core, part),
+                code_send.at[part], code_recv.at[part], to_near,
+            )
+        )
 
     zero = jnp.zeros((), BF16)
     lane_c = lax.broadcasted_iota(jnp.int32, (2 * chunks, 2 * TPL), 1)
@@ -513,7 +526,8 @@
         region = other_region(i)
 
         def store(where, value):
-            rest_stat[where] = jnp.where(rest_reg[...] == region, value, rest_stat[where])
+            at = slice(where * 2 * TPL, (where + 1) * 2 * TPL)
+            stat_ref[hot_pad:, at] = jnp.where(rest_reg[...] == region, value, stat_ref[hot_pad:, at])
 
         finish_list(rest_pad, rest_close.at[at], rest_sum.at[at], rest_total.at[at], store)
 
@@ -527,16 +541,19 @@
     split_rest = kept == banks - 1
     sides = [(side, hops) for hops in range(1, banks) for side in range(2)]
     every = [(0, 0)] + sides
-    work = [functools.partial(codes, part) for part in range(2 * banks)]
+    work = [functools.partial(codes, part) for part in range(banks)]
 
     def some(count=1):
         for _ in range(min(count, len(work))):
             work.pop(0)()
 
+    pl.semaphore_wait(barrier, met)
+    send_own()
+    for copy in small:
+        copy.wait()
     fill_tables()
     fill_power()
-    pl.semaphore_wait(barrier, met)
-    send_own()
+    send_power()
     fill_turns()
     pick_lists()
     fill_lhs(seg, lambda c, d: strain_ref[c, d * rec : (d + 1) * rec, :])
@@ -574,7 +591,10 @@
     some(len(work))
     landed(strain_all.at[far_near], str_recv.at[2])
     fill_lhs(far_near, landed_strain(far_near))
+    send_codes(banks - 1)
     pow_relay(P_X)
+    for part in range(banks):
+        landed(codes_at(core_near, part), code_recv.at[part])
     for side, hops in every:
         for kind in (N_MINE, N_OTHER):
             relay(kind, side, hops)
@@ -601,12 +621,12 @@
     for side, hops in every:
         for kind in (N_FAR_MINE, N_FAR_OTHER):
             relay(kind, side, hops)
-    rest_stat[...] = jnp.zeros_like(rest_stat)
+    stat_ref[...] = jnp.zeros_like(stat_ref)
 
     hot_half(1)
 
-    def store_hot(at, value):
-        hot_stat[at] = value
+    def store_hot(where, value):
+        stat_ref[:hot_pad, where * 2 * TPL : (where + 1) * 2 * TPL] = value
 
     finish_list(hot_pad, hot_close, hot_sum, hot_total, store_hot)
     if split_rest:
@@ -622,15 +642,14 @@
 
         each_other(whole_region)
 
+    placed = lax.dot_general(
+        jnp.concatenate([hot_sel[...], rest_sel[...]], axis=0), stat_ref[...], TN,
+        precision=HIGH, preferred_element_type=F32,
+    )
     for which, out_ref in enumerate((snr_ref, chi_ref)):
         for lag in range(lags):
-            at = which * lags + lag
-            value = lax.dot_general(
-                hot_sel[...], hot_stat[at], TN, precision=HIGH, preferred_element_type=F32
-            ) + lax.dot_general(
-                rest_sel[...], rest_stat[at], TN, precision=HIGH, preferred_element_type=F32
-            )
-            out_ref[lag] = value[:, :TPL]
+            at = (which * lags + lag) * 2 * TPL
+            out_ref[lag] = placed[:, at : at + TPL]
     for finish in started:
         finish()
 
@@ -1178,14 +1197,15 @@
             pltpu.VMEM((kept, 2, rows_rest, 2 * TPL), F32),
             pltpu.VMEM((kept, 2, rows_rest, 2 * TPL), F32),
             pltpu.VMEM((kept, rows_rest, 2 * TPL), F32),
-            pltpu.VMEM((2 * lags, hot_pad, 2 * TPL), F32),
-            pltpu.VMEM((2 * lags, rest_pad, 2 * TPL), F32),
+            pltpu.VMEM((hot_pad + rest_pad, 2 * lags * 2 * TPL), F32),
             dma((9, 2 * region_count)),
             dma((9, 2 * region_count)),
             dma((4, 2 * region_count)),
             dma((4, 2 * region_count)),
             dma((3,)),
             dma((3,)),
+            dma((region_count,)),
+            dma((region_count,)),
             dma((6,)),
         ],
         compiler_params=pltpu.CompilerParams(

time: 35.1 us -> 33.6 us (0.957)
  Pallas kernels: 30.3 us -> 28.8 us
    pallas_call x1, Pallas kernels: 30.3 us -> 28.8 us  [per_device(): pl.pallas_call(functools.partial(follow_up_kernel, cap, rec, hot_pad, res...]
where the time goes in v3:
time: 33.6 us; the launch traced here: 33.4 us
  Pallas kernels  28.8 us (86%)
  local copies, waits for them, and re-layouts  3.11 us (9%)
  between operations  1.21 us (4%)
    pallas_call x1, Pallas kernels, per_device(): pl.pallas_call(functools.partial(follow_up_kernel, cap, rec, hot_pad, res...  28.8 us
    unnamed x2, local copies, waits for them, and re-layouts  1.26 us
    transpose x1, local copies, waits for them, and re-layouts, per_device(): jnp.transpose(strain, (2, 1, 0, 3)).reshape(2, 2 * rec, width)  0.93 us
    transpose x1, local copies, waits for them, and re-layouts, per_device(): jnp.transpose(templates, (1, 0, 2))  0.92 us

profile of v3, /device:TPU:0, one launch (start us, length us, event | category | flops | bytes accessed | tf_op | source)
XLA Modules:
  0.0 33.4 jit_solution(16221458320208889072)
XLA Ops:
  0.6 0.9 %copy.19 = bf16[2,64,512]{2,1,0:T(8,128)(2,1)S(1)} copy(bf16[2,64,512]{2,0,1:T(2,128)(2,1)} %bitcast.23) | data formatting | bytes 262144 | tf_op jit(solution)/shard_map/transpose | solution.py:1148
  1.6 0.9 %copy.20 = bf16[2,2,32,512]{3,2,1,0:T(8,128)(2,1)S(1)} copy(bf16[2,2,32,512]{3,0,1,2:T(2,128)(2,1)} %bitcast.24) | data formatting | bytes 262144 | tf_op jit(solution)/shard_map/transpose | solution.py:1149
  2.5 28.8 %follow_up.1 = (f32[4,32,64]{2,1,0:T(8,128)S(1)}, f32[4,32,64]{2,1,0:T(8,128)S(1)}, s32[1]{0:T(128)}) custom-call(bf16[2,4,16,512]{3,2,1,0:T(8,128)(2,1)S(1)} %bitcast.21, bf16[2,64,512]{2,1,0:T(8,128)(2,1)S(1)} %bitcast.22, s32[1,32]{1,0:T(1,128)} %bitcast.31, s32[15,256]{1,0:T(8,128)} %bitcast.25, s32[4,4]{1,0:T(4,128)} %reads_hbm.1), custom_call_target="tpu_custom_call" | custom-call | tf_op jit(solution)/shard_map/follow_up/pallas_call | solution.py:1165
  31.9 0.2 conditional.1
  32.1 0.6 %copy.31 = f32[4,64,32]{1,2,0:T(8,128)} copy(f32[4,64,32]{1,2,0:T(8,128)S(1)} %get-tuple-element.84) | data formatting | bytes 65536
  32.7 0.6 %copy.32 = f32[4,64,32]{1,2,0:T(8,128)} copy(f32[4,64,32]{1,2,0:T(8,128)S(1)} %get-tuple-element.85) | data formatting | bytes 65536

commit v4 on v3

--- a/solution.py
+++ b/solution.py
@@ -606,18 +606,13 @@
     for side in range(2):
         relay(Y_FAR, side, 1)
     hot_half(0)
-    for hops in range(2, banks - 1):
+    relay(X_OTHER)
+    for hops in range(2, banks):
         for side in range(2):
             relay(Y_FAR, side, hops)
     if split_rest:
-        for i in range(1, banks - 1):
+        for i in range(1, banks):
             rest_half(0, i, i - 1)
-    relay(X_OTHER)
-    if banks > 2:
-        for side in range(2):
-            relay(Y_FAR, side, banks - 1)
-    if split_rest:
-        rest_half(0, banks - 1, banks - 2)
     for side, hops in every:
         for kind in (N_FAR_MINE, N_FAR_OTHER):
             relay(kind, side, hops)

time: 33.6 us -> 32.7 us (0.973)
  Pallas kernels: 28.8 us -> 27.9 us
    pallas_call x1, Pallas kernels: 28.8 us -> 27.9 us  [per_device(): pl.pallas_call(functools.partial(follow_up_kernel, cap, rec, hot_pad, res...]
where the time goes in v4:
time: 32.7 us; the launch traced here: 32.4 us
  Pallas kernels  27.9 us (85%)
  local copies, waits for them, and re-layouts  3.11 us (10%)
  between operations  1.21 us (4%)
    pallas_call x1, Pallas kernels, per_device(): pl.pallas_call(functools.partial(follow_up_kernel, cap, rec, hot_pad, res...  27.9 us
    unnamed x2, local copies, waits for them, and re-layouts  1.26 us
    transpose x1, local copies, waits for them, and re-layouts, per_device(): jnp.transpose(strain, (2, 1, 0, 3)).reshape(2, 2 * rec, width)  0.93 us
    transpose x1, local copies, waits for them, and re-layouts, per_device(): jnp.transpose(templates, (1, 0, 2))  0.92 us

profile of v4, /device:TPU:0, one launch (start us, length us, event | category | flops | bytes accessed | tf_op | source)
XLA Modules:
  0.0 32.4 jit_solution(12773052394623634166)
XLA Ops:
  0.6 0.9 %copy.19 = bf16[2,64,512]{2,1,0:T(8,128)(2,1)S(1)} copy(bf16[2,64,512]{2,0,1:T(2,128)(2,1)} %bitcast.23) | data formatting | bytes 262144 | tf_op jit(solution)/shard_map/transpose | solution.py:1143
  1.6 0.9 %copy.20 = bf16[2,2,32,512]{3,2,1,0:T(8,128)(2,1)S(1)} copy(bf16[2,2,32,512]{3,0,1,2:T(2,128)(2,1)} %bitcast.24) | data formatting | bytes 262144 | tf_op jit(solution)/shard_map/transpose | solution.py:1144
  2.5 27.9 %follow_up.1 = (f32[4,32,64]{2,1,0:T(8,128)S(1)}, f32[4,32,64]{2,1,0:T(8,128)S(1)}, s32[1]{0:T(128)}) custom-call(bf16[2,4,16,512]{3,2,1,0:T(8,128)(2,1)S(1)} %bitcast.21, bf16[2,64,512]{2,1,0:T(8,128)(2,1)S(1)} %bitcast.22, s32[1,32]{1,0:T(1,128)} %bitcast.31, s32[15,256]{1,0:T(8,128)} %bitcast.25, s32[4,4]{1,0:T(4,128)} %reads_hbm.1), custom_call_target="tpu_custom_call" | custom-call | tf_op jit(solution)/shard_map/follow_up/pallas_call | solution.py:1160
  30.9 0.2 conditional.1
  31.1 0.6 %copy.31 = f32[4,64,32]{1,2,0:T(8,128)} copy(f32[4,64,32]{1,2,0:T(8,128)S(1)} %get-tuple-element.84) | data formatting | bytes 65536
  31.8 0.6 %copy.32 = f32[4,64,32]{1,2,0:T(8,128)} copy(f32[4,64,32]{1,2,0:T(8,128)S(1)} %get-tuple-element.85) | data formatting | bytes 65536
